TPU v7x, 128 devices: a whole 4x4x4 slice. The times are simulated.
128 devices in a mesh: dp: 8 (over z, core), sp: 16 (over y, x).
Axes of the slice: x: 4, y: 4, z: 4, core: 2. Of those that a mesh axis runs over, the one named last changes fastest.
Arguments:
- projected: bfloat16 [16384, 10240], P(('dp', 'sp')), may hold values from -4 to 4
- bias: float32 [10240], replicated, may hold values from -3 to 3
- cotangent: bfloat16 [16384, 8192], P(('dp', 'sp')), may hold values from -4 to 4
- lengths: int32 [8, 4], P('dp'), may hold values from 1 to 1024, 2048 in all within a row
- page_source: int32 [8, 128], P('dp'), may hold values from 0 to 127, as said below
Outputs:
- attended: bfloat16 [16384, 8192], P(('dp', 'sp'))
- grad_query: bfloat16 [16384, 8192], P(('dp', 'sp'))
- key_value_gradient: bfloat16 [16384, 2048], P(('dp', 'sp'))
- grad_bias: float32 [10240], replicated
Inputs may be any that keep to these rules, and one draw needn't show every extreme that they name: Each row holds the lengths of the 4 sequences of one group in packed order and sums to 2048; the longest is exactly 1024. `page_source`: rollout page r of a group lies on the group's device r // 8 at slot r % 8. Each row is a permutation of the group's pages, and no device sends two pages to the same device of its group.
All inputs are finite; a program needn't handle non-finite values.
Results may differ from a plain program's by a relative error of at most 0.012.
Values may be sent and summed in bfloat16 or wider, within the bound.
No kernel may reach another device: no remote copies, remote signals or barrier semaphores. Data moves between devices by JAX's collectives and lax.ppermute only.
A program may use at most 192 MiB of HBM per device.

v0:
```python
import jax
import jax.numpy as jnp
from jax import lax
from jax.sharding import PartitionSpec as P

QUERY_HEADS = 64
KEY_VALUE_HEADS = 8
HEAD_DIMENSION = 128
PAGE = 16
QBLK = 512


rope_base = 1000000.0


def rope_tables(positions, head_size):
    half_size = head_size // 2
    exponent = jnp.arange(half_size, dtype=jnp.float32) * 2.0 / head_size
    frequency = jnp.power(jnp.float32(rope_base), -exponent)
    angles = positions.astype(jnp.float32)[:, None] * frequency[None, :]
    cosine_table = jnp.cos(angles)
    sine_table = jnp.sin(angles)
    return (
        jnp.concatenate([cosine_table, cosine_table], 1),
        jnp.concatenate([sine_table, sine_table], 1),
    )


def turn_half(tensor_in):
    half_size = tensor_in.shape[-1] // 2
    return jnp.concatenate([-tensor_in[..., half_size:], tensor_in[..., :half_size]], -1)


def apply_rotary(tensor_in, cosine_table, sine_table):
    return tensor_in * cosine_table[:, None, :] + turn_half(tensor_in) * sine_table[:, None, :]


def unrotate(tensor_in, cosine_table, sine_table):
    return tensor_in * cosine_table[:, None, :] - turn_half(tensor_in) * sine_table[:, None, :]


def segments_of(seq_lengths, token_total_count):
    seq_ends = jnp.cumsum(seq_lengths)
    seq_starts = seq_ends - seq_lengths
    tokens_at = jnp.arange(token_total_count, dtype=jnp.int32)
    segment = jnp.sum((tokens_at[:, None] >= seq_ends[None, :]).astype(jnp.int32), 1)
    labels = jnp.arange(seq_lengths.shape[0], dtype=jnp.int32)
    first_token = jnp.sum(jnp.where(segment[:, None] == labels[None, :], seq_starts[None, :], 0), 1)
    return (segment, tokens_at - first_token, first_token)


def shards(projected, bias, cotangent, lengths, page_source):
    shard_rows, row_width = projected.shape
    partition_count = lax.axis_size("sp")
    my_index = lax.axis_index("sp")
    group_rows = shard_rows * partition_count
    pages_dev = shard_rows // PAGE
    query_span_width = QUERY_HEADS * HEAD_DIMENSION
    key_value_width = KEY_VALUE_HEADS * HEAD_DIMENSION
    heads_dev = QUERY_HEADS // partition_count
    head_copies = partition_count // KEY_VALUE_HEADS
    page_table = page_source[0]
    page_grid = page_table.reshape(partition_count, pages_dev)
    source_dev = page_grid // pages_dev
    source_slot = page_grid % pages_dev
    from_here = source_dev == my_index
    pick_slot = jnp.sum(jnp.where(from_here, source_slot, 0), 1)
    present = jnp.any(from_here, 1)
    local_pages = projected.reshape(pages_dev, PAGE, row_width)
    outgoing = jnp.where(
        present[:, None, None], local_pages[pick_slot], jnp.zeros((), projected.dtype)
    )
    incoming = lax.all_to_all(outgoing, "sp", split_axis=0, concat_axis=0, tiled=True)
    own_sources = lax.dynamic_slice_in_dim(source_dev, my_index, 1, 0)[0]
    trainer_rows = incoming[own_sources].reshape(shard_rows, row_width)
    query_part = trainer_rows[:, :query_span_width]
    key_part = trainer_rows[:, query_span_width : query_span_width + key_value_width].reshape(
        shard_rows, KEY_VALUE_HEADS, 1, HEAD_DIMENSION
    )
    value_portion = trainer_rows[:, query_span_width + key_value_width :].reshape(
        shard_rows, KEY_VALUE_HEADS, 1, HEAD_DIMENSION
    )
    joined_rows = jnp.concatenate([key_part, value_portion], 3)
    repeated_heads = jnp.broadcast_to(
        joined_rows, (shard_rows, KEY_VALUE_HEADS, head_copies, 2 * HEAD_DIMENSION)
    ).reshape(shard_rows, partition_count * 2 * HEAD_DIMENSION)
    head_query, head_pair, head_upstream = (
        lax.all_to_all(query_part, "sp", split_axis=1, concat_axis=0, tiled=True),
        lax.all_to_all(repeated_heads, "sp", split_axis=1, concat_axis=0, tiled=True),
        lax.all_to_all(cotangent, "sp", split_axis=1, concat_axis=0, tiled=True),
    )
    kv_head = my_index // head_copies
    query_bias = lax.dynamic_slice_in_dim(
        bias, my_index * heads_dev * HEAD_DIMENSION, heads_dev * HEAD_DIMENSION
    )
    key_bias = lax.dynamic_slice_in_dim(
        bias, query_span_width + kv_head * HEAD_DIMENSION, HEAD_DIMENSION
    )
    value_bias = lax.dynamic_slice_in_dim(
        bias, query_span_width + key_value_width + kv_head * HEAD_DIMENSION, HEAD_DIMENSION
    )
    segment, position, first_token = segments_of(lengths[0], group_rows)
    cosine_table, sine_table = rope_tables(position, HEAD_DIMENSION)
    query_matrix = head_query.astype(jnp.float32).reshape(
        group_rows, heads_dev, HEAD_DIMENSION
    ) + query_bias.reshape(heads_dev, HEAD_DIMENSION)
    query_matrix = apply_rotary(query_matrix, cosine_table, sine_table).astype(jnp.bfloat16)
    key_rows = head_pair[:, :HEAD_DIMENSION].astype(jnp.float32) + key_bias
    key_rows = apply_rotary(key_rows[:, None, :], cosine_table, sine_table)[:, 0].astype(
        jnp.bfloat16
    )
    value_rows = (head_pair[:, HEAD_DIMENSION:].astype(jnp.float32) + value_bias).astype(
        jnp.bfloat16
    )
    block_count = group_rows // QBLK
    score_scale = HEAD_DIMENSION ** (-0.5)
    query_blocks = query_matrix.reshape(block_count, QBLK, heads_dev, HEAD_DIMENSION)
    key_blocks = key_rows.reshape(block_count, QBLK, HEAD_DIMENSION)
    value_blocks = value_rows.reshape(block_count, QBLK, HEAD_DIMENSION)
    segment_blocks = segment.reshape(block_count, QBLK)
    token_blocks = jnp.arange(group_rows, dtype=jnp.int32).reshape(block_count, QBLK)
    upstream_gradient = head_upstream.reshape(block_count, QBLK, heads_dev, HEAD_DIMENSION)

    def weights(row_block, col_block):
        scores = (
            jnp.einsum(
                "qhd,kd->hqk",
                query_blocks[row_block],
                key_blocks[col_block],
                preferred_element_type=jnp.float32,
            )
            * score_scale
        )
        keep = (segment_blocks[row_block][:, None] == segment_blocks[col_block][None, :]) & (
            token_blocks[row_block][:, None] >= token_blocks[col_block][None, :]
        )
        return jnp.where(keep[None], jnp.exp(scores), 0.0)

    zero_rows = jnp.zeros((heads_dev, QBLK), jnp.float32)
    totals = []
    for row_block in range(block_count):
        running = zero_rows
        for col_block in range(row_block + 1):
            running = running + jnp.sum(weights(row_block, col_block), 2)
        totals.append(running)
    zero_out = jnp.zeros((QBLK, heads_dev, HEAD_DIMENSION), jnp.float32)
    attended_blocks = []
    for row_block in range(block_count):
        running = zero_out
        for col_block in range(row_block + 1):
            attend_probs = (weights(row_block, col_block) / totals[row_block][:, :, None]).astype(
                jnp.bfloat16
            )
            running = running + jnp.einsum(
                "hqk,kd->qhd",
                attend_probs,
                value_blocks[col_block],
                preferred_element_type=jnp.float32,
            )
        attended_blocks.append(running.astype(jnp.bfloat16))
    attended = jnp.stack(attended_blocks)
    attended_out = lax.all_to_all(
        attended.reshape(group_rows, heads_dev * HEAD_DIMENSION),
        "sp",
        split_axis=0,
        concat_axis=1,
        tiled=True,
    )
    zero_key = jnp.zeros((QBLK, HEAD_DIMENSION), jnp.float32)
    key_grads = [zero_key for col_block in range(block_count)]
    value_grads = [zero_key for col_block in range(block_count)]
    query_grads = []
    for row_block in range(block_count):
        delta = jnp.transpose(
            jnp.sum(
                upstream_gradient[row_block].astype(jnp.float32)
                * attended[row_block].astype(jnp.float32),
                2,
            )
        )
        running = zero_out
        for col_block in range(row_block + 1):
            probs = weights(row_block, col_block) / totals[row_block][:, :, None]
            rounded = probs.astype(jnp.bfloat16)
            dprobs = jnp.einsum(
                "qhd,kd->hqk",
                upstream_gradient[row_block],
                value_blocks[col_block],
                preferred_element_type=jnp.float32,
            )
            dscores = (probs * (dprobs - delta[:, :, None])).astype(jnp.bfloat16)
            part_query = (
                jnp.einsum(
                    "hqk,kd->qhd",
                    dscores,
                    key_blocks[col_block],
                    preferred_element_type=jnp.float32,
                )
                * score_scale
            )
            part_key = (
                jnp.einsum(
                    "hqk,qhd->kd",
                    dscores,
                    query_blocks[row_block],
                    preferred_element_type=jnp.float32,
                )
                * score_scale
            )
            part_value = jnp.einsum(
                "hqk,qhd->kd",
                rounded,
                upstream_gradient[row_block],
                preferred_element_type=jnp.float32,
            )
            part_query, part_key, part_value = (part_query, part_key, part_value)
            running = running + part_query
            key_grads[col_block] = key_grads[col_block] + part_key
            value_grads[col_block] = value_grads[col_block] + part_value
        query_grads.append(running)
    rot_query = jnp.stack(query_grads).reshape(group_rows, heads_dev, HEAD_DIMENSION)
    grad_query = (
        unrotate(rot_query, cosine_table, sine_table)
        .astype(jnp.bfloat16)
        .reshape(group_rows, heads_dev * HEAD_DIMENSION)
    )
    query_out = lax.all_to_all(grad_query, "sp", split_axis=0, concat_axis=1, tiled=True)
    grad_key = unrotate(
        jnp.stack(key_grads).reshape(group_rows, 1, HEAD_DIMENSION), cosine_table, sine_table
    ).reshape(group_rows, HEAD_DIMENSION)
    grad_value = jnp.stack(value_grads).reshape(group_rows, HEAD_DIMENSION)
    pair_grads = jnp.concatenate([grad_key, grad_value], 1)
    pair_gradient_back = lax.all_to_all(pair_grads, "sp", split_axis=0, concat_axis=1, tiled=True)
    pair_gradient_sum = jnp.sum(
        pair_gradient_back.reshape(shard_rows, KEY_VALUE_HEADS, head_copies, 2, HEAD_DIMENSION), 2
    )
    key_value_gradient = (
        jnp.transpose(pair_gradient_sum, (0, 2, 1, 3))
        .reshape(shard_rows, 2 * key_value_width)
        .astype(jnp.bfloat16)
    )
    local_sums = jnp.concatenate(
        [
            jnp.sum(query_out.astype(jnp.float32), 0),
            jnp.sum(key_value_gradient.astype(jnp.float32), 0),
        ]
    )
    grad_bias = lax.psum(local_sums, ("dp", "sp"))
    return (attended_out, query_out, key_value_gradient, grad_bias)


def solution(mesh):
    in_specs = (P(("dp", "sp"), None), P(), P(("dp", "sp"), None), P("dp", None), P("dp", None))
    out_specs = (P(("dp", "sp"), None), P(("dp", "sp"), None), P(("dp", "sp"), None), P())
    return jax.shard_map(shards, mesh=mesh, in_specs=in_specs, out_specs=out_specs, check_vma=False)
```

profile of v0, /device:TPU:64, one launch (start us, length us, event | category | flops | bytes accessed | tf_op | source)
XLA Modules:
  0.0 490.8 jit_solution(9390538019138670282)
XLA Ops:
  3.1 3.2 gather_fusion
  6.4 5.3 %broadcast_select_fusion = bf16[16,16,10240]{2,1,0:T(8,128)(2,1)} fusion(bf16[16,16,10240]{2,1,0:T(8,128)(2,1)} %gather_fusion, pred[16]{0:T(512)(128)(4,1)S(1)} %get-tuple-element.28), kind=kLoop, calls=%fused_computation.2 | loop fusion | flops 2621440 | bytes 10485776 | tf_op jit(solution)/shard_map/jit(_where)/select_n | solution.py:70
  11.6 7.2 %all-to-all-start = ((bf16[16,16,10240]{2,1,0:T(8,128)(2,1)}), bf16[16,16,10240]{2,1,0:T(8,128)(2,1)}, u32[]{:S(2)}, u32[]{:S(2)}) async-start(bf16[16,16,10240]{2,1,0:T(8,128)(2,1)} %broadcast_select_fusion), calls=%async_computation | async-start | bytes 10485760 | tf_op jit(solution)/shard_map/all_to_all | solution.py:73
  19.0 2.4 copy.566
  21.6 75.5 %all-to-all-done = bf16[16,16,10240]{2,1,0:T(8,128)(2,1)} async-done(((bf16[16,16,10240]{2,1,0:T(8,128)(2,1)}), bf16[16,16,10240]{2,1,0:T(8,128)(2,1)}, u32[]{:S(2)}, u32[]{:S(2)}) %all-to-all-start) | async-done | bytes 5242912 | tf_op jit(solution)/shard_map/all_to_all | solution.py:73
  97.1 5.4 %all-to-all-start.4 = ((bf16[128,16,512]{0,2,1:T(8,128)(2,1)}), bf16[128,16,512]{0,2,1:T(8,128)(2,1)}, u32[]{:S(2)}, u32[]{:S(2)}) async-start(bf16[128,16,512]{0,2,1:T(8,128)(2,1)} %bitcast.61), calls=%async_computation.4 | async-start | bytes 4194304 | tf_op jit(solution)/shard_map/all_to_all | solution.py:90
  102.6 5.5 %multiply_cosine_fusion.1 = (f32[2048,64]{1,0:T(8,128)}, f32[2048,64]{1,0:T(8,128)}) fusion(f32[64]{0:T(128)S(1)} %negate_power_fusion, f32[2048]{0:T(1024)S(1)} %subtract_convert_fusion.1), kind=kLoop, calls=%fused_computation.79 | loop fusion | flops 131072 | bytes 1057024 | tf_op jit(solution)/shard_map/cos | solution.py:21
  108.2 3.2 gather_fusion.1
  111.7 20.4 %all-to-all-done.4 = bf16[128,16,512]{0,2,1:T(8,128)(2,1)} async-done(((bf16[128,16,512]{0,2,1:T(8,128)(2,1)}), bf16[128,16,512]{0,2,1:T(8,128)(2,1)}, u32[]{:S(2)}, u32[]{:S(2)}) %all-to-all-start.4) | async-done | bytes 2097184 | tf_op jit(solution)/shard_map/all_to_all | solution.py:90
  133.2 4.3 all-to-all-start.1
  137.6 5.5 %multiply_sine_fusion = (f32[16,128,64]{2,1,0:T(8,128)}, f32[16,128,64]{2,1,0:T(8,128)}) fusion(f32[64]{0:T(128)S(1)} %negate_power_fusion, f32[16,128]{1,0:T(8,128)S(1)} %fusion.135), kind=kLoop, calls=%fused_computation.76 | loop fusion | flops 131072 | bytes 1057024 | tf_op jit(solution)/shard_map/sin | solution.py:22
  143.2 3.4 compare_and_fusion.9
  148.1 4.1 copy.541
  152.2 1.7 all-to-all-done.1
  153.8 5.7 %all-to-all-start.2 = ((bf16[128,16,512]{0,2,1:T(8,128)(2,1)}), bf16[128,16,512]{0,2,1:T(8,128)(2,1)}, u32[]{:S(2)}, u32[]{:S(2)}) async-start(bf16[128,16,512]{0,2,1:T(8,128)(2,1)} %bitcast.21), calls=%async_computation.2 | async-start | bytes 4194304 | tf_op jit(solution)/shard_map/all_to_all | solution.py:88
  161.1 1.7 fusion.165
  169.9 3.5 fusion.77
  173.4 2.4 mul.272.clone
  175.8 5.4 %reshape.962 = f32[16,128,512]{2,1,0:T(8,128)} reshape(f32[2048,4,128]{2,1,0:T(4,128)} %mul.272.clone) | data formatting | bytes 8388608 | tf_op jit(solution)/shard_map/mul | solution.py:35
  181.3 6.8 %all-to-all-done.2 = bf16[128,16,512]{0,2,1:T(8,128)(2,1)} async-done(((bf16[128,16,512]{0,2,1:T(8,128)(2,1)}), bf16[128,16,512]{0,2,1:T(8,128)(2,1)}, u32[]{:S(2)}, u32[]{:S(2)}) %all-to-all-start.2) | async-done | bytes 2097184 | tf_op jit(solution)/shard_map/all_to_all | solution.py:88
  188.0 2.0 convert_bitcast_fusion
  190.1 4.4 copy.542
  194.5 5.0 %reshape.897 = f32[2048,4,128]{0,2,1:T(8,128)} reshape(f32[16,128,512]{1,0,2:T(8,128)} %copy.542) | data formatting | bytes 8388608 | tf_op jit(solution)/shard_map/convert_element_type | solution.py:104
  199.5 5.7 %copy.543 = f32[2048,4,128]{2,0,1:T(8,128)} copy(f32[2048,4,128]{0,2,1:T(8,128)} %reshape.897) | data formatting | bytes 8388608 | tf_op jit(solution)/shard_map/convert_element_type | solution.py:104
  205.2 2.5 broadcast_add_fusion
  209.8 2.8 fusion.1
  212.7 2.5 fusion.37
  219.0 1.8 convolution_bitcast_fusion.6
  220.7 1.8 convolution_bitcast_fusion
  222.5 1.8 convolution_bitcast_fusion.3
  243.4 1.8 convolution_bitcast_fusion.7
  245.2 1.8 convolution_bitcast_fusion.4
  251.2 2.8 fusion.11
  255.6 1.7 fusion.27
  259.9 1.8 convolution_bitcast_fusion.8
  263.0 2.9 fusion.17
  273.7 1.9 fusion.74
  278.5 1.6 convolution_bitcast_fusion.18
  284.7 1.8 pad_maximum_fusion.1
  286.5 4.3 copy.564
  290.8 4.1 all_to_all.82
  294.9 4.6 all-to-all-start.3
  299.5 2.4 fusion.65
  302.0 2.5 fusion.62
  304.6 1.9 fusion.58
  322.1 6.5 %all-to-all-done.3 = bf16[16,128,512]{2,1,0:T(8,128)(2,1)} async-done(((bf16[16,128,512]{2,1,0:T(8,128)(2,1)}), bf16[16,128,512]{2,1,0:T(8,128)(2,1)}, u32[]{:S(2)}, u32[]{:S(2)}) %all-to-all-start.3) | async-done | bytes 2097184 | tf_op jit(solution)/shard_map/all_to_all | solution.py:162
  328.6 4.6 all-to-all-start.6
  333.3 4.2 pad_maximum_fusion
  337.4 5.3 %copy.604 = f32[4,512,4,128]{3,1,0,2:T(8,128)} copy(f32[4,512,4,128]{1,3,2,0:T(8,128)} %pad_maximum_fusion) | data formatting | bytes 8388608 | tf_op jit(solution)/shard_map/stack | solution.py:221
  342.7 5.2 %copy.601 = f32[4,512,4,128]{3,2,1,0:T(4,128)} copy(f32[4,512,4,128]{1,3,2,0:T(8,128)} %pad_maximum_fusion) | data formatting | bytes 8388608 | tf_op jit(solution)/shard_map/stack | solution.py:221
  348.0 5.6 %reshape.892 = f32[16,128,512]{2,1,0:T(8,128)} reshape(f32[4,512,4,128]{3,2,1,0:T(4,128)} %copy.601) | data formatting | bytes 8388608 | tf_op jit(solution)/shard_map/reshape | solution.py:221
  353.5 4.9 %slice_negate_fusion = (f32[2048,4,64]{2,0,1:T(8,128)S(1)}, f32[2048,4,64]{2,0,1:T(8,128)S(1)}) fusion(f32[2048,4,128]{2,0,1:T(8,128)} %bitcast.579), kind=kLoop, calls=%fused_computation.3 | loop fusion | flops 524288 | bytes 8388608 | tf_op jit(solution)/shard_map/neg | solution.py:31
  359.6 10.0 %copy.704 = f32[2048,4,128]{2,1,0:T(4,128)} copy(f32[2048,4,128]{2,0,1:T(8,128)S(1)} %maximum_multiply_fusion.1) | data formatting | bytes 8388608 | tf_op jit(solution)/shard_map/mul | solution.py:39
  369.6 5.5 %reshape.963 = f32[16,128,512]{2,1,0:T(8,128)} reshape(f32[2048,4,128]{2,1,0:T(4,128)} %copy.704) | data formatting | bytes 8388608 | tf_op jit(solution)/shard_map/mul | solution.py:39
  375.1 7.2 %subtract_convert_fusion = bf16[16,128,512]{2,1,0:T(8,128)(2,1)} fusion(f32[16,128,512]{2,1,0:T(8,128)} %reshape.963, f32[16,128,512]{2,1,0:T(8,128)} %reshape.892, f32[16,128,512]{2,1,0:T(8,128)} %reshape.962), kind=kLoop, calls=%fused_computation.52 | loop fusion | flops 3145728 | bytes 14680064 | tf_op jit(solution)/shard_map/convert_element_type | solution.py:224
  382.3 7.5 %all-to-all-start.5 = ((bf16[16,128,512]{2,1,0:T(8,128)(2,1)}), bf16[16,128,512]{2,1,0:T(8,128)(2,1)S(1)}, u32[]{:S(2)}, u32[]{:S(2)}) async-start(bf16[16,128,512]{2,1,0:T(8,128)(2,1)} %subtract_convert_fusion), calls=%async_computation.5 | async-start | bytes 4194304 | tf_op jit(solution)/shard_map/all_to_all | solution.py:227
  389.8 3.9 copy.565
  393.7 4.1 copy.620
  397.8 3.2 reshape.896
  401.0 3.3 reduce_sum.209
  406.3 12.1 %all-to-all-done.5 = bf16[16,128,512]{2,1,0:T(8,128)(2,1)S(1)} async-done(((bf16[16,128,512]{2,1,0:T(8,128)(2,1)}), bf16[16,128,512]{2,1,0:T(8,128)(2,1)S(1)}, u32[]{:S(2)}, u32[]{:S(2)}) %all-to-all-start.5) | async-done | bytes 2097184 | tf_op jit(solution)/shard_map/all_to_all | solution.py:227
  420.1 62.1 %psum.7 = f32[10240]{0:T(1024)} all-reduce(f32[10240]{0:T(1024)S(1)} %pad_maximum_fusion.7), channel_id=1, replica_groups=mesh['dp'=8,'sp'=16] {'dp','sp'}, use_global_device_ids=true, to_apply=%region_22.23 | all-reduce | flops 10240 | bytes 81920 | tf_op jit(solution)/shard_map/psum | solution.py:248
  482.2 4.1 copy.607
  486.3 4.1 copy.621
  (219 shorter events, 84.5 us)
Async XLA Ops:
  0.6 2.5 copy-start
  11.6 7.2 %copy-start.49 = (s32[1,4]{1,0:T(1,128)S(1)}, s32[1,4]{1,0:T(1,128)}, u32[]{:S(2)}) copy-start(s32[1,4]{1,0:T(1,128)} %param.8) | copy-start | bytes 52
  11.6 7.4 %copy-start.16 = (bf16[128,8192]{1,0:T(8,128)(2,1)S(1)}, bf16[128,8192]{1,0:T(8,128)(2,1)}, u32[]{:S(2)}) copy-start(bf16[128,8192]{1,0:T(8,128)(2,1)} %param.7) | copy-start | bytes 6291460
  11.6 85.5 %all-to-all-start = ((bf16[16,16,10240]{2,1,0:T(8,128)(2,1)}), bf16[16,16,10240]{2,1,0:T(8,128)(2,1)}, u32[]{:S(2)}, u32[]{:S(2)}) async-start(bf16[16,16,10240]{2,1,0:T(8,128)(2,1)} %broadcast_select_fusion), calls=%async_computation | async-start | bytes 10485760 | tf_op jit(solution)/shard_map/all_to_all | solution.py:73
  97.1 35.0 %all-to-all-start.4 = ((bf16[128,16,512]{0,2,1:T(8,128)(2,1)}), bf16[128,16,512]{0,2,1:T(8,128)(2,1)}, u32[]{:S(2)}, u32[]{:S(2)}) async-start(bf16[128,16,512]{0,2,1:T(8,128)(2,1)} %bitcast.61), calls=%async_computation.4 | async-start | bytes 4194304 | tf_op jit(solution)/shard_map/all_to_all | solution.py:90
  133.2 20.6 %all-to-all-start.1 = ((bf16[128,16,256]{2,0,1:T(8,128)(2,1)}), bf16[128,16,256]{2,0,1:T(8,128)(2,1)}, u32[]{:S(2)}, u32[]{:S(2)}) async-start(bf16[128,16,256]{2,0,1:T(8,128)(2,1)} %bitcast.588), calls=%async_computation.1 | async-start | bytes 2097152 | tf_op jit(solution)/shard_map/all_to_all | solution.py:89
  153.8 34.2 %all-to-all-start.2 = ((bf16[128,16,512]{0,2,1:T(8,128)(2,1)}), bf16[128,16,512]{0,2,1:T(8,128)(2,1)}, u32[]{:S(2)}, u32[]{:S(2)}) async-start(bf16[128,16,512]{0,2,1:T(8,128)(2,1)} %bitcast.21), calls=%async_computation.2 | async-start | bytes 4194304 | tf_op jit(solution)/shard_map/all_to_all | solution.py:88
  173.4 35.6 %copy-start.4 = (f32[2048,128]{1,0:T(8,128)}, f32[2048,128]{1,0:T(8,128)S(1)}, u32[]{:S(2)}) copy-start(f32[2048,128]{1,0:T(8,128)S(1)} %get-tuple-element.45) | copy-start | bytes 3145732
  207.6 2.2 copy-start.2
  212.7 2.5 copy-start.10
  212.7 2.5 copy-start.44
  215.2 1.3 copy-start.43
  217.7 1.3 copy-start.30
  220.7 1.8 copy-start.45
  235.4 36.8 %copy-start.17 = (bf16[4,512,512]{1,2,0:T(8,128)(2,1)}, bf16[4,512,512]{1,2,0:T(8,128)(2,1)S(1)}, u32[]{:S(2)}) copy-start(bf16[4,512,512]{1,2,0:T(8,128)(2,1)S(1)} %fusion.3) | copy-start | bytes 6291460
  237.6 1.7 copy-start.38
  239.3 1.5 copy-start.40
  242.1 1.3 copy-start.29
  251.2 25.8 %copy-start.19 = (bf16[4,512,512]{1,2,0:T(8,128)(2,1)}, bf16[4,512,512]{1,2,0:T(8,128)(2,1)S(1)}, u32[]{:S(2)}) copy-start(bf16[4,512,512]{1,2,0:T(8,128)(2,1)S(1)} %fusion.13) | copy-start | bytes 6291460
  254.0 1.5 copy-start.36
  255.5 20.0 %copy-start.21 = (bf16[4,512,512]{1,2,0:T(8,128)(2,1)}, bf16[4,512,512]{1,2,0:T(8,128)(2,1)S(1)}, u32[]{:S(2)}) copy-start(bf16[4,512,512]{1,2,0:T(8,128)(2,1)S(1)} %fusion.15) | copy-start | bytes 6291460
  255.5 1.7 copy-start.39
  257.3 5.7 %copy-start.50 = (f32[512,512,4]{1,0,2:T(8,128)}, f32[512,512,4]{1,0,2:T(8,128)S(1)}, u32[]{:S(2)}) copy-start(f32[512,512,4]{1,0,2:T(8,128)S(1)} %get-tuple-element.90) | copy-start | bytes 12582916
  258.5 1.3 copy-start.27
  267.4 11.1 %copy-start.23 = (bf16[4,512,512]{1,2,0:T(8,128)(2,1)}, bf16[4,512,512]{1,2,0:T(8,128)(2,1)S(1)}, u32[]{:S(2)}) copy-start(bf16[4,512,512]{1,2,0:T(8,128)(2,1)S(1)} %fusion.19) | copy-start | bytes 6291460
  275.6 4.5 copy-start.34
  278.4 2.8 copy-start.25
  281.3 2.0 copy-start.52
  284.7 19.8 %copy-start.6 = (bf16[4,512,512]{1,2,0:T(8,128)(2,1)}, bf16[4,512,512]{1,2,0:T(8,128)(2,1)S(1)}, u32[]{:S(2)}) copy-start(bf16[4,512,512]{1,2,0:T(8,128)(2,1)S(1)} %fusion.21) | copy-start | bytes 6291460
  290.8 8.7 %copy-start.33 = (f32[512,128]{1,0:T(8,128)S(1)}, f32[512,128]{1,0:T(8,128)}, u32[]{:S(2)}) copy-start(f32[512,128]{1,0:T(8,128)} %convolution_bitcast_fusion.11) | copy-start | bytes 786436
  294.9 7.1 %copy-start.47 = (f32[512,128]{1,0:T(8,128)S(1)}, f32[512,128]{1,0:T(8,128)}, u32[]{:S(2)}) copy-start(f32[512,128]{1,0:T(8,128)} %convolution_bitcast_fusion.13) | copy-start | bytes 786436
  294.9 33.7 %all-to-all-start.3 = ((bf16[16,128,512]{2,1,0:T(8,128)(2,1)}), bf16[16,128,512]{2,1,0:T(8,128)(2,1)}, u32[]{:S(2)}, u32[]{:S(2)}) async-start(bf16[16,128,512]{2,1,0:T(8,128)(2,1)} %all_to_all.82), calls=%async_computation.3 | async-start | bytes 4194304 | tf_op jit(solution)/shard_map/all_to_all | solution.py:162
  299.5 5.0 %copy-start.31 = (f32[512,128]{1,0:T(8,128)S(1)}, f32[512,128]{1,0:T(8,128)}, u32[]{:S(2)}) copy-start(f32[512,128]{1,0:T(8,128)} %convolution_bitcast_fusion.17) | copy-start | bytes 786436
  299.5 5.0 %copy-start.32 = (f32[512,128]{1,0:T(8,128)S(1)}, f32[512,128]{1,0:T(8,128)}, u32[]{:S(2)}) copy-start(f32[512,128]{1,0:T(8,128)} %convolution_bitcast_fusion.18) | copy-start | bytes 786436
  302.0 4.5 copy-start.48
  304.5 2.4 copy-start.28
  304.5 2.4 copy-start.37
  304.5 2.6 copy-start.51
  304.6 2.6 copy-start.57
  304.6 2.6 copy-start.58
  307.2 1.3 copy-start.26
  307.2 1.3 copy-start.35
  307.2 2.4 copy-start.53
  307.2 2.4 copy-start.54
  307.2 2.5 copy-start.55
  307.2 2.6 copy-start.56
  309.8 1.2 copy-start.46
  309.8 1.4 copy-start.11
  309.8 1.7 copy-start.12
  311.5 2.4 copy-start.7
  312.4 2.9 copy-start.13
  312.4 2.9 copy-start.18
  313.9 2.9 copy-start.22
  315.3 2.1 copy-start.20
  316.8 1.7 copy-start.8
  317.4 2.5 copy-start.24
  318.6 2.1 copy-start.9
  320.6 12.6 %copy-start.14 = (f32[1,512,4,128]{1,3,2,0:T(8,128)S(1)}, f32[1,512,4,128]{1,3,2,0:T(8,128)}, u32[]{:S(2)}) copy-start(f32[1,512,4,128]{1,3,2,0:T(8,128)} %fusion.42) | copy-start | bytes 3145732
  322.1 11.1 %copy-start.15 = (f32[1,512,4,128]{1,3,2,0:T(8,128)S(1)}, f32[1,512,4,128]{1,3,2,0:T(8,128)}, u32[]{:S(2)}) copy-start(f32[1,512,4,128]{1,3,2,0:T(8,128)} %fusion.48) | copy-start | bytes 3145732
  328.6 53.7 %all-to-all-start.6 = ((f32[16,128,256]{2,1,0:T(8,128)}), f32[16,128,256]{2,1,0:T(8,128)}, u32[]{:S(2)}, u32[]{:S(2)}) async-start(f32[16,128,256]{2,1,0:T(8,128)} %pad_maximum_fusion.2), calls=%async_computation.6 | async-start | bytes 4194304 | tf_op jit(solution)/shard_map/all_to_all | solution.py:233
  353.5 4.9 %copy-start.5 = (f32[2048,128]{1,0:T(8,128)S(1)}, f32[2048,128]{1,0:T(8,128)}, u32[]{:S(2)}) copy-start(f32[2048,128]{1,0:T(8,128)} %copy-done.4) | copy-start | bytes 3145732
  382.3 36.1 %all-to-all-start.5 = ((bf16[16,128,512]{2,1,0:T(8,128)(2,1)}), bf16[16,128,512]{2,1,0:T(8,128)(2,1)S(1)}, u32[]{:S(2)}, u32[]{:S(2)}) async-start(bf16[16,128,512]{2,1,0:T(8,128)(2,1)} %subtract_convert_fusion), calls=%async_computation.5 | async-start | bytes 4194304 | tf_op jit(solution)/shard_map/all_to_all | solution.py:227
  418.4 1.3 copy-start.3
  482.2 8.1 %copy-start.1 = (bf16[128,10240]{1,0:T(8,128)(2,1)S(1)}, bf16[128,10240]{1,0:T(8,128)(2,1)}, u32[]{:S(2)}) copy-start(bf16[128,10240]{1,0:T(8,128)(2,1)} %param.5) | copy-start | bytes 7864324
  (2 other events, 2.4 us)
where the time goes:
time: 499 us; the launch traced here: 491 us
  waiting for transfers between devices  123 us (25%)
  local copies, waits for them, and re-layouts  115 us (23%)
  matrix products  87.4 us (18%)
  blocking collectives  62.1 us (12%)
  other arithmetic  61.9 us (12%)
  starting transfers between devices  39.3 us (8%)
    all_to_all x1, waiting for transfers between devices, shards(): lax.all_to_all(outgoing, 'sp', split_axis=0, concat_axis=0, tiled=True)  75.5 us
    psum x1, blocking collectives, shards(): grad_bias = lax.psum(local_sums, ('dp', 'sp'))  62.1 us
    all_to_all x1, waiting for transfers between devices, shards(): lax.all_to_all(cotangent, 'sp', split_axis=1, concat_axis=0, tiled=True)  20.4 us
    unnamed x127, local copies, waits for them, and re-layouts  18.1 us
    dot_general x10, matrix products, shards(): jnp.einsum('qhd,kd->hqk', upstream_gradient[row_block], value_blocks[col_...  17.7 us
    dot_general x10, matrix products, shards(): jnp.einsum('hqk,qhd->kd', dscores, query_blocks[row_block], preferred_ele...  16.3 us
    dot_general x10, matrix products, shards(): jnp.einsum('hqk,qhd->kd', rounded, upstream_gradient[row_block], preferre...  16.1 us
    mul x2, local copies, waits for them, and re-layouts, unrotate(): turn_half(tensor_in) * sine_table[:, None, :]  15.5 us
  transfers between devices with their start and end apart: 7, of which 6 were waited for; matrix products, arithmetic and copies ran while one was open for 27% of the time, Pallas kernels for 0%

commit v1 on v0

v1 whole, which is shorter than its diff:
```python
import functools

import jax
import jax.numpy as jnp
from jax import lax
from jax.experimental import pallas as pl
from jax.experimental.pallas import tpu as pltpu
from jax.sharding import PartitionSpec as P

QUERY_HEADS = 64
KEY_VALUE_HEADS = 8
HEAD = 128
PAGE = 16
BLK = 256
SCALE = HEAD ** (-0.5)
LOG2E = 1.4426950408889634
NEG = -1e30
ROPE_BASE = 1000000.0
VMEM_BYTES = 60 * 1024 * 1024
EXTRA = 8

BF = jnp.bfloat16
F32 = jnp.float32
ANY = pl.BlockSpec(memory_space=pl.ANY)
VM = pl.BlockSpec(memory_space=pltpu.VMEM)
SM = pl.BlockSpec(memory_space=pltpu.SMEM)


def params():
    return pltpu.CompilerParams(vmem_limit_bytes=VMEM_BYTES)


def cost(flops, nbytes):
    return pl.CostEstimate(flops=flops, bytes_accessed=nbytes, transcendentals=0)


def run_copies(copies):
    for copy in copies:
        copy.start()
    for copy in copies:
        copy.wait()


def pack_kernel(chunk, ways, proj, cot, out, sem):
    kv0 = QUERY_HEADS * HEAD
    copies = []

    def add(src, dst):
        copies.append(pltpu.make_async_copy(src, dst, sem.at[len(copies)]))

    copies_of = ways // KEY_VALUE_HEADS
    for d in range(ways):
        col = d * 512 + chunk * 256
        add(proj.at[:, pl.ds(col, 256)], out.at[d, :, pl.ds(0, 256)])
        add(cot.at[:, pl.ds(col, 256)], out.at[d, :, pl.ds(256, 256)])
        if chunk == 0:
            kcol = kv0 + (d // copies_of) * HEAD
            vcol = kcol + KEY_VALUE_HEADS * HEAD
            add(proj.at[:, pl.ds(kcol, HEAD)], out.at[d, :, pl.ds(512, HEAD)])
            add(proj.at[:, pl.ds(vcol, HEAD)], out.at[d, :, pl.ds(640, HEAD)])
    run_copies(copies)


def pack(chunk, ways, proj, cot):
    rows = proj.shape[0]
    width = 768 if chunk == 0 else 512
    return pl.pallas_call(
        functools.partial(pack_kernel, chunk, ways),
        out_shape=jax.ShapeDtypeStruct((ways, rows, width), BF),
        in_specs=[ANY, ANY],
        out_specs=VM,
        scratch_shapes=[pltpu.SemaphoreType.DMA((ways * (4 if chunk == 0 else 2),))],
        compiler_params=params(),
        cost_estimate=cost(0, 4 * ways * rows * width),
        name=f"pack{chunk}",
    )(proj, cot)


def rope(x, c, s):
    return x * c + pltpu.roll(x, HEAD // 2, 1) * s


def unrope(g, c, s):
    return g * c - pltpu.roll(g, HEAD // 2, 1) * s


def keys_kernel(page, kv, bias, cos, sin, k_out, v_out, kt_out, vt_out):
    kb = bias[0:1, :]
    vb = bias[1:2, :]
    npages = kv.shape[0] // PAGE

    def one(p, _):
        src = pl.ds(pl.multiple_of(page[p] * PAGE, PAGE), PAGE)
        dst = pl.ds(pl.multiple_of(p * PAGE, PAGE), PAGE)
        k = kv[src, 0:HEAD].astype(F32) + kb
        v = kv[src, HEAD : 2 * HEAD].astype(F32) + vb
        k_out[dst, :] = rope(k, cos[dst, :], sin[dst, :]).astype(BF)
        v_out[dst, :] = v.astype(BF)
        return 0

    lax.fori_loop(0, npages, one, 0, unroll=4)

    def turn(b, _):
        rows = pl.ds(pl.multiple_of(b * BLK, BLK), BLK)
        kt_out[:, rows] = jnp.transpose(k_out[rows, :].astype(F32)).astype(BF)
        vt_out[:, rows] = jnp.transpose(v_out[rows, :].astype(F32)).astype(BF)
        return 0

    lax.fori_loop(0, kv.shape[0] // BLK, turn, 0)


def make_keys(page, recv, bias, cos, sin):
    n = recv.shape[0]
    row = jax.ShapeDtypeStruct((n, HEAD), BF)
    col = jax.ShapeDtypeStruct((HEAD, n), BF)
    return pl.pallas_call(
        keys_kernel,
        grid=(1,),
        out_shape=(row, row, col, col),
        in_specs=[
            SM,
            pl.BlockSpec((n, 256), lambda i: (0, 2)),
            VM,
            VM,
            VM,
        ],
        out_specs=(VM, VM, VM, VM),
        compiler_params=params(),
        cost_estimate=cost(4 * 10**9, 6 * n * 256),
        name="keys",
    )(page, recv, bias, cos, sin)


def attend_kernel(
    last, first_block, page, qd, k, v, kt, vt, cos, sin, first, qbias, dk_in, dv_in, sums_in,
    out, dk, dv, sums, qs, st, ot, dqt,
):
    n = k.shape[0]
    blocks = n // BLK
    per = BLK // 128
    bias = [qbias[0:1, :], qbias[1:2, :]]

    def gather(p, _):
        src = pl.ds(pl.multiple_of(page[p] * PAGE, PAGE), PAGE)
        dst = pl.ds(pl.multiple_of(p * PAGE, PAGE), PAGE)
        c, s = cos[dst, :], sin[dst, :]
        base = (p // (BLK // PAGE)) * (2 * BLK) + (p % (BLK // PAGE)) * PAGE
        for h in range(2):
            x = qd[src, h * HEAD : (h + 1) * HEAD].astype(F32) + bias[h]
            qs[pl.ds(pl.multiple_of(base + h * BLK, PAGE), PAGE), :] = rope(x, c, s).astype(BF)
        return 0

    lax.fori_loop(0, n // PAGE, gather, 0, unroll=4)
    if last:
        dk[...] = dk_in[...]
        dv[...] = dv_in[...]
    else:
        dk[...] = jnp.zeros_like(dk)
        dv[...] = jnp.zeros_like(dv)

    nt = (((1,), (1,)), ((), ()))
    nn = (((1,), (0,)), ((), ()))

    def block(i, carry):
        rows = pl.ds(pl.multiple_of(i * BLK, BLK), BLK)
        q = qs[pl.ds(pl.multiple_of(i * 2 * BLK, 2 * BLK), 2 * BLK), :]
        do = jnp.concatenate([qd[rows, 256:384], qd[rows, 384:512]], 0)
        lo = first_block[i]
        start1 = first[0:1, rows]
        start = jnp.concatenate([start1, start1], 1)
        lane = lax.broadcasted_iota(jnp.int32, (1, BLK), 1) + i * BLK
        token = jnp.concatenate([lane, lane], 1)

        def score(j, m):
            cols = pl.ds(pl.multiple_of(j * BLK, BLK), BLK)
            s = lax.dot_general(k[cols, :], q, nt, preferred_element_type=F32) * (SCALE * LOG2E)
            key = lax.broadcasted_iota(jnp.int32, (BLK, 2 * BLK), 0) + j * BLK
            s = jnp.where((key <= token) & (key >= start), s, NEG)
            st[j - lo] = s
            return jnp.maximum(m, jnp.max(s, 0, keepdims=True))

        m = lax.fori_loop(lo, i + 1, score, jnp.full((1, 2 * BLK), NEG, F32))

        def expo(j, total):
            e = jnp.exp2(st[j - lo] - m)
            st[j - lo] = e
            return total + jnp.sum(e, 0, keepdims=True)

        total = lax.fori_loop(lo, i + 1, expo, jnp.zeros((1, 2 * BLK), F32))
        inv = 1.0 / total
        ot[...] = jnp.zeros_like(ot)

        def value(j, _):
            cols = pl.ds(pl.multiple_of(j * BLK, BLK), BLK)
            p = st[j - lo] * inv
            st[j - lo] = p
            ot[...] += lax.dot_general(vt[:, cols], p.astype(BF), nn, preferred_element_type=F32)
            return 0

        lax.fori_loop(lo, i + 1, value, 0)
        o_t = ot[...].astype(BF).astype(F32)
        do_t = jnp.transpose(do.astype(F32))
        delta = jnp.sum(o_t * do_t, 0, keepdims=True)
        dqt[...] = jnp.zeros_like(dqt)

        def back(j, _):
            cols = pl.ds(pl.multiple_of(j * BLK, BLK), BLK)
            p = st[j - lo]
            dp = lax.dot_general(v[cols, :], do, nt, preferred_element_type=F32)
            ds = (p * (dp - delta)).astype(BF)
            dv[cols, :] += lax.dot_general(p.astype(BF), do, nn, preferred_element_type=F32)
            dk[cols, :] += lax.dot_general(ds, q, nn, preferred_element_type=F32)
            dqt[...] += lax.dot_general(kt[:, cols], ds, nn, preferred_element_type=F32)
            return 0

        lax.fori_loop(lo, i + 1, back, 0)
        o = jnp.transpose(o_t).astype(BF)
        dq = jnp.transpose(dqt[...]) * SCALE
        c, s = cos[rows, :], sin[rows, :]
        new = []
        for h in range(2):
            g = unrope(dq[h * BLK : (h + 1) * BLK], c, s).astype(BF)
            new.append(carry[h] + jnp.sum(g.astype(F32), 0, keepdims=True))
            for a in range(per):
                part = slice(a * 128, (a + 1) * 128)
                out[i * per + a, 0:128, h * HEAD : (h + 1) * HEAD] = o[h * BLK + a * 128 : h * BLK + (a + 1) * 128]
                out[i * per + a, 0:128, 256 + h * HEAD : 256 + (h + 1) * HEAD] = g[part]
        return tuple(new)

    zero = jnp.zeros((1, HEAD), F32)
    head_sums = lax.fori_loop(0, blocks, block, (zero, zero))
    if not last:
        sums[...] = jnp.zeros_like(sums)
        sums[0:1, :] = head_sums[0]
        sums[1:2, :] = head_sums[1]
        return

    def finish(b, carry):
        rows = pl.ds(pl.multiple_of(b * 128, 128), 128)
        gk = unrope(dk[rows, :] * SCALE, cos[rows, :], sin[rows, :])
        gv = dv[rows, :]
        out[b, 0:128, 512:640] = gk.astype(BF)
        out[b, 0:128, 640:768] = gv.astype(BF)
        return (
            carry[0] + jnp.sum(gk, 0, keepdims=True),
            carry[1] + jnp.sum(gv, 0, keepdims=True),
        )

    kv_sums = lax.fori_loop(0, n // 128, finish, (zero, zero))
    sums[...] = sums_in[...]
    sums[2:3, :] = head_sums[0]
    sums[3:4, :] = head_sums[1]
    sums[4:5, :] = kv_sums[0]
    sums[5:6, :] = kv_sums[1]


def attend(last, ways, first_block, page, recv, keys, cos, sin, first, qbias, dk, dv, sums):
    n = recv.shape[0]
    k, v, kt, vt = keys
    rows, width = (128 + EXTRA, 768) if last else (128, 512)
    grad = jax.ShapeDtypeStruct((n, HEAD), F32)
    return pl.pallas_call(
        functools.partial(attend_kernel, last),
        grid=(1,),
        out_shape=(
            jax.ShapeDtypeStruct((ways, rows, width), BF),
            grad,
            grad,
            jax.ShapeDtypeStruct((8, HEAD), F32),
        ),
        in_specs=[SM, SM, pl.BlockSpec((n, 512), lambda i: (0, 0))] + [VM] * 11,
        out_specs=(VM, VM, VM, VM),
        scratch_shapes=[
            pltpu.VMEM((2 * n, HEAD), BF),
            pltpu.VMEM((1024 // BLK + 1, BLK, 2 * BLK), F32),
            pltpu.VMEM((HEAD, 2 * BLK), F32),
            pltpu.VMEM((HEAD, 2 * BLK), F32),
        ],
        compiler_params=params(),
        cost_estimate=cost(20 * 10**9, 10**7),
        name="attend1" if last else "attend0",
    )(first_block, page, recv, k, v, kt, vt, cos, sin, first, qbias, dk, dv, sums)


def sums_kernel(sums, _, out, rows, sem):
    for r in range(6):
        x = sums[r : r + 1, :]
        hi = x.astype(BF).astype(F32)
        mid = (x - hi).astype(BF).astype(F32)
        low = x - hi - mid
        rows[:, r * HEAD : (r + 1) * HEAD] = jnp.concatenate(
            [hi, mid, low, jnp.zeros((EXTRA - 3, HEAD), F32)], 0
        ).astype(BF)
    run_copies(
        [
            pltpu.make_async_copy(rows, out.at[d, pl.ds(128, EXTRA), :], sem.at[d])
            for d in range(out.shape[0])
        ]
    )


def put_sums(sums, payload):
    ways = payload.shape[0]
    return pl.pallas_call(
        sums_kernel,
        out_shape=jax.ShapeDtypeStruct(payload.shape, payload.dtype),
        in_specs=[VM, ANY],
        out_specs=ANY,
        input_output_aliases={1: 0},
        scratch_shapes=[pltpu.VMEM((EXTRA, 768), BF), pltpu.SemaphoreType.DMA((ways,))],
        compiler_params=params(),
        name="sums",
    )(sums, payload)


def unpack0_kernel(recv, att, gq, sem):
    copies = []
    for d in range(recv.shape[0]):
        cols = pl.ds(d * 512, 256)
        copies.append(pltpu.make_async_copy(recv.at[d, :, pl.ds(0, 256)], att.at[:, cols], sem.at[2 * d]))
        copies.append(pltpu.make_async_copy(recv.at[d, :, pl.ds(256, 256)], gq.at[:, cols], sem.at[2 * d + 1]))
    run_copies(copies)


def unpack0(recv):
    ways, rows, _ = recv.shape
    shape = jax.ShapeDtypeStruct((rows, QUERY_HEADS * HEAD), BF)
    return pl.pallas_call(
        unpack0_kernel,
        out_shape=(shape, shape),
        in_specs=[VM],
        out_specs=(ANY, ANY),
        scratch_shapes=[pltpu.SemaphoreType.DMA((2 * ways,))],
        compiler_params=params(),
        cost_estimate=cost(0, 4 * ways * rows * 512),
        name="unpack0",
    )(recv)


def unpack1_kernel(recv, _a, _g, att, gq, kvg, gb, sem):
    copies = []
    ways = recv.shape[0]
    for d in range(ways):
        cols = pl.ds(d * 512 + 256, 256)
        copies.append(
            pltpu.make_async_copy(recv.at[d, pl.ds(0, 128), pl.ds(0, 256)], att.at[:, cols], sem.at[2 * d])
        )
        copies.append(
            pltpu.make_async_copy(recv.at[d, pl.ds(0, 128), pl.ds(256, 256)], gq.at[:, cols], sem.at[2 * d + 1])
        )
    for copy in copies:
        copy.start()
    share = ways // KEY_VALUE_HEADS
    qw = QUERY_HEADS * HEAD
    kw = KEY_VALUE_HEADS * HEAD

    def sums_of(d):
        t = recv[d, 128 : 128 + EXTRA, :].astype(F32)
        return t[0:1] + t[1:2] + t[2:3]

    for h in range(KEY_VALUE_HEADS):
        grad = jnp.zeros((128, 256), F32)
        kvsum = jnp.zeros((1, 256), F32)
        for r in range(share):
            d = h * share + r
            grad = grad + recv[d, 0:128, 512:768].astype(F32)
            b = sums_of(d)
            gb[:, d * 512 : (d + 1) * 512] = b[:, 0:512]
            kvsum = kvsum + b[:, 512:768]
        kvg[:, h * HEAD : (h + 1) * HEAD] = grad[:, :HEAD].astype(BF)
        kvg[:, kw + h * HEAD : kw + (h + 1) * HEAD] = grad[:, HEAD:].astype(BF)
        gb[:, qw + h * HEAD : qw + (h + 1) * HEAD] = kvsum[:, :HEAD]
        gb[:, qw + kw + h * HEAD : qw + kw + (h + 1) * HEAD] = kvsum[:, HEAD:]
    for copy in copies:
        copy.wait()


def unpack1(recv, att, gq):
    ways = recv.shape[0]
    rows = att.shape[0]
    return pl.pallas_call(
        unpack1_kernel,
        out_shape=(
            jax.ShapeDtypeStruct(att.shape, BF),
            jax.ShapeDtypeStruct(gq.shape, BF),
            jax.ShapeDtypeStruct((rows, 2 * KEY_VALUE_HEADS * HEAD), BF),
            jax.ShapeDtypeStruct((1, (QUERY_HEADS + 2 * KEY_VALUE_HEADS) * HEAD), F32),
        ),
        in_specs=[VM, ANY, ANY],
        out_specs=(ANY, ANY, VM, VM),
        input_output_aliases={1: 0, 2: 1},
        scratch_shapes=[pltpu.SemaphoreType.DMA((2 * ways,))],
        compiler_params=params(),
        cost_estimate=cost(0, 4 * ways * rows * 768),
        name="unpack1",
    )(recv, att, gq)


def rope_tables(positions):
    lane = jnp.arange(HEAD, dtype=jnp.int32)
    exponent = (lane % (HEAD // 2)).astype(F32) * 2.0 / HEAD
    frequency = jnp.power(jnp.float32(ROPE_BASE), -exponent)
    angles = positions.astype(F32)[:, None] * frequency[None, :]
    sign = jnp.where(lane < HEAD // 2, -1.0, 1.0).astype(F32)
    return jnp.cos(angles), jnp.sin(angles) * sign[None, :]


def exchange(x):
    return lax.all_to_all(x, "sp", split_axis=0, concat_axis=0, tiled=True)


def shards(projected, bias, cotangent, lengths, page_source):
    ways = lax.axis_size("sp")
    me = lax.axis_index("sp")
    rows = projected.shape[0]
    n = rows * ways
    page = page_source[0]
    recv0 = exchange(pack(0, ways, projected, cotangent))
    recv1 = exchange(pack(1, ways, projected, cotangent))

    ends = jnp.cumsum(lengths[0])
    starts = ends - lengths[0]
    tokens = jnp.arange(n, dtype=jnp.int32)
    first = jnp.max(jnp.where(tokens[:, None] >= starts[None, :], starts[None, :], 0), 1)
    first_block = first.reshape(n // BLK, BLK)[:, 0] // BLK
    cos, sin = rope_tables(tokens - first)
    first = first[None, :]

    qw = QUERY_HEADS * HEAD
    kw = KEY_VALUE_HEADS * HEAD
    kv_head = me // (ways // KEY_VALUE_HEADS)
    bias_rows = bias.reshape(-1, HEAD)
    qbias = lax.dynamic_slice_in_dim(bias_rows, me * 4, 4)
    kvbias = jnp.stack([bias_rows[QUERY_HEADS + kv_head], bias_rows[QUERY_HEADS + KEY_VALUE_HEADS + kv_head]])

    flat0 = recv0.reshape(n, 768)
    keys = make_keys(page, flat0, kvbias, cos, sin)
    none = jnp.zeros((8, HEAD), F32)
    send2, dk, dv, sums = attend(
        False, ways, first_block, page, flat0, keys, cos, sin, first, qbias[0:2], none, none, none
    )
    recv2 = exchange(send2)
    send3, _, _, sums = attend(
        True, ways, first_block, page, recv1.reshape(n, 512), keys, cos, sin, first, qbias[2:4], dk, dv, sums
    )
    sums = lax.psum(sums, "dp")
    recv3 = exchange(put_sums(sums, send3))
    att, gq = unpack0(recv2)
    att, gq, kvg, gb = unpack1(recv3, att, gq)
    return att, gq, kvg, gb.reshape(-1)


def solution(mesh):
    in_specs = (P(("dp", "sp"), None), P(), P(("dp", "sp"), None), P("dp", None), P("dp", None))
    out_specs = (P(("dp", "sp"), None), P(("dp", "sp"), None), P(("dp", "sp"), None), P())
    return jax.shard_map(shards, mesh=mesh, in_specs=in_specs, out_specs=out_specs, check_vma=False)
```

time: 499 us -> 226 us (0.45); the launches traced: 491 us -> 224 us
  local copies, waits for them, and re-layouts: 115 us -> 5.72 us
  Pallas kernels: 0 us -> 88.9 us
  matrix products: 87.4 us -> 0 us
  other arithmetic: 61.9 us -> 7.03 us
  blocking collectives: 62.1 us -> 12 us
  waiting for transfers between devices: 123 us -> 84.2 us
  starting transfers between devices: 39.3 us -> 25.5 us
    pallas_call x0 -> x8, Pallas kernels: none -> 88.9 us  [the longest x2 66 us: attend(): pl.pallas_call(functools.partial(attend_kernel, last), grid=(1,), out_sha...]
    dot_general x60 -> x0, matrix products: 87.4 us -> none  [the longest x10 17.7 us: shards(): jnp.einsum('qhd,kd->hqk', upstream_gradient[row_block], value_blocks[col_...]
    psum x1, blocking collectives: 62.1 us -> 12 us  [shards(): sums = lax.psum(sums, 'dp')]
    all_to_all x7 -> x4, waiting for transfers between devices: 123 us -> 84.2 us  [exchange(): return lax.all_to_all(x, 'sp', split_axis=0, concat_axis=0, tiled=True)]
    mul x4 -> x0, local copies, waits for them, and re-layouts: 23.3 us -> none  [the longest x2 15.5 us: unrotate(): turn_half(tensor_in) * sine_table[:, None, :]]
    convert_element_type x6 -> x1, other arithmetic: 15.6 us -> 0.01 us  [rope_tables(): angles = positions.astype(F32)[:, None] * frequency[None, :]]
    convert_element_type x4 -> x0, local copies, waits for them, and re-layouts: 15.6 us -> none  [the longest x3 15.1 us: shards(): head_query.astype(jnp.float32)]
    unnamed x127 -> x10, local copies, waits for them, and re-layouts: 18.1 us -> 3.07 us
  transfers between devices with their start and end apart: 7 -> 4, of which waited for: 6 -> 2; matrix products, arithmetic and copies ran while one was open for 27% -> 4% of each run, Pallas kernels for 0% -> 36%
where the time goes in v1:
time: 226 us; the launch traced here: 224 us
  Pallas kernels  88.9 us (39%)
  waiting for transfers between devices  84.2 us (37%)
  starting transfers between devices  25.5 us (11%)
  blocking collectives  12 us (5%)
  other arithmetic  7.03 us (3%)
  local copies, waits for them, and re-layouts  5.72 us (3%)
    all_to_all x4, waiting for transfers between devices, exchange(): return lax.all_to_all(x, 'sp', split_axis=0, concat_axis=0, tiled=True)  84.2 us
    pallas_call x2, Pallas kernels, attend(): pl.pallas_call(functools.partial(attend_kernel, last), grid=(1,), out_sha...  66 us
    all_to_all x4, starting transfers between devices, exchange(): return lax.all_to_all(x, 'sp', split_axis=0, concat_axis=0, tiled=True)  25.5 us
    psum x1, blocking collectives, shards(): sums = lax.psum(sums, 'dp')  12 us
    pallas_call x2, Pallas kernels, pack(): pl.pallas_call(functools.partial(pack_kernel, chunk, ways), out_shape=jax...  7.31 us
    pallas_call x1, Pallas kernels, make_keys(): pl.pallas_call(keys_kernel, grid=(1,), out_shape=(row, row, col, col), in...  6.62 us
    mul x1, other arithmetic, rope_tables(): return (jnp.cos(angles), jnp.sin(angles) * sign[None, :])  5.62 us
  transfers between devices with their start and end apart: 4, of which 2 were waited for; matrix products, arithmetic and copies ran while one was open for 4% of the time, Pallas kernels for 36%

profile of v1, /device:TPU:64, one launch (start us, length us, event | category | flops | bytes accessed | tf_op | source)
XLA Modules:
  0.0 224.3 jit_solution(129616293285149820)
XLA Ops:
  0.6 4.1 %pack0.1 = bf16[16,128,768]{2,1,0:T(8,128)(2,1)} custom-call(bf16[128,10240]{1,0:T(8,128)(2,1)} %proj.3, bf16[128,8192]{1,0:T(8,128)(2,1)} %cot.3), custom_call_target="tpu_custom_call" | custom-call | bytes 6291456 | tf_op jit(solution)/shard_map/pack0/pallas_call | solution.py:67
  4.8 7.0 %all-to-all-start.1 = ((bf16[16,128,768]{2,1,0:T(8,128)(2,1)}), bf16[16,128,768]{2,1,0:T(8,128)(2,1)S(1)}, u32[]{:S(2)}, u32[]{:S(2)}) async-start(bf16[16,128,768]{2,1,0:T(8,128)(2,1)} %pack0.1), calls=%async_computation.1 | async-start | bytes 6291456 | tf_op jit(solution)/shard_map/all_to_all | solution.py:409
  11.8 0.0 copy-start.4
  11.8 3.2 %pack1.1 = bf16[16,128,512]{2,1,0:T(8,128)(2,1)} custom-call(bf16[128,10240]{1,0:T(8,128)(2,1)} %proj.3, bf16[128,8192]{1,0:T(8,128)(2,1)} %cot.3), custom_call_target="tpu_custom_call" | custom-call | bytes 4194304 | tf_op jit(solution)/shard_map/pack1/pallas_call | solution.py:67
  15.0 0.0 copy-done.4
  15.1 0.2 reduce-window_clone.1
  15.2 0.1 select_reduce_fusion
  15.3 0.0 copy-start.3
  15.4 0.7 constant_dynamic-slice_fusion.2
  16.1 0.6 pad_maximum_fusion.bias
  16.7 0.7 constant_dynamic-slice_fusion
  17.4 0.1 slice_reduce_fusion
  17.5 0.5 and_select_fusion.1.first_block
  18.0 0.5 fusion.5
  18.6 5.6 %fusion = (f32[2048,128]{1,0:T(8,128)}, f32[2048,128]{1,0:T(8,128)}) fusion(f32[128]{0:T(128)S(1)} %get-tuple-element.42, f32[128]{0:T(128)S(1)} %get-tuple-element.43, f32[2048]{0:T(1024)S(1)} %subtract_convert_fusion), kind=kLoop, calls=%fused_computation.2 | loop fusion | flops 524288 | bytes 2106368 | tf_op jit(solution)/shard_map/mul | solution.py:405
  24.2 35.3 %all-to-all-done.1 = bf16[16,128,768]{2,1,0:T(8,128)(2,1)S(1)} async-done(((bf16[16,128,768]{2,1,0:T(8,128)(2,1)}), bf16[16,128,768]{2,1,0:T(8,128)(2,1)S(1)}, u32[]{:S(2)}, u32[]{:S(2)}) %all-to-all-start.1) | async-done | bytes 3145760 | tf_op jit(solution)/shard_map/all_to_all | solution.py:409
  59.5 0.0 copy-start.2
  59.5 0.0 copy-done.3
  59.5 4.4 %all-to-all-start = ((bf16[16,128,512]{2,1,0:T(8,128)(2,1)}), bf16[16,128,512]{2,1,0:T(8,128)(2,1)}, u32[]{:S(2)}, u32[]{:S(2)}) async-start(bf16[16,128,512]{2,1,0:T(8,128)(2,1)} %pack1.1), calls=%async_computation | async-start | bytes 4194304 | tf_op jit(solution)/shard_map/all_to_all | solution.py:409
  63.9 0.0 copy-done.2
  63.9 6.6 %keys.1 = (bf16[2048,128]{1,0:T(8,128)(2,1)}, bf16[2048,128]{1,0:T(8,128)(2,1)}, bf16[128,2048]{1,0:T(8,128)(2,1)}, bf16[128,2048]{1,0:T(8,128)(2,1)}) custom-call(s32[128]{0:T(128)} %bitcast.15, bf16[2048,768]{1,0:T(8,128)(2,1)} %bitcast.8, f32[2,128]{1,0:T(2,128)} %pad_maximum_fusion.bias, f32[2048,128]{1,0:T(8,128)} %get-tuple-element.39.cos, ...), custom_call_target="tpu_custom_call" | custom-call | flops 4000000000 | bytes 3145728 | tf_op jit(solution)/shard_map/keys/pallas_call | solution.py:116
  70.5 0.6 broadcast_in_dim.34.dk_in.dv_in.sums_in
  71.1 31.6 %attend0.1 = (bf16[16,128,512]{2,1,0:T(8,128)(2,1)}, f32[2048,128]{1,0:T(8,128)}, f32[2048,128]{1,0:T(8,128)}, f32[8,128]{1,0:T(8,128)}) custom-call(s32[8]{0:T(128)} %and_select_fusion.1.first_block, s32[128]{0:T(128)} %bitcast.16, bf16[2048,768]{1,0:T(8,128)(2,1)} %bitcast.9, bf16[2048,128]{1,0:T(8,128)(2,1)} %get-tuple-element.20.k, ...), custom_call_target="tpu_custom_call" | custom-call | flops 20000000000 | bytes 10000000 | tf_op jit(solution)/shard_map/attend0/pallas_call | solution.py:262
  102.7 0.0 all-to-all-done
  102.7 7.1 %all-to-all-start.3 = ((bf16[16,128,512]{2,1,0:T(8,128)(2,1)}), bf16[16,128,512]{2,1,0:T(8,128)(2,1)S(1)}, u32[]{:S(2)}, u32[]{:S(2)}) async-start(bf16[16,128,512]{2,1,0:T(8,128)(2,1)} %get-tuple-element.29), calls=%async_computation.3 | async-start | bytes 4194304 | tf_op jit(solution)/shard_map/all_to_all | solution.py:409
  109.9 34.4 %attend1.1 = (bf16[16,136,768]{2,1,0:T(8,128)(2,1)}, f32[2048,128]{1,0:T(8,128)}, f32[2048,128]{1,0:T(8,128)}, f32[8,128]{1,0:T(8,128)}) custom-call(s32[8]{0:T(128)} %and_select_fusion.1.first_block, s32[128]{0:T(128)} %bitcast.17, bf16[2048,512]{1,0:T(8,128)(2,1)} %bitcast.2.qd, bf16[2048,128]{1,0:T(8,128)(2,1)} %get-tuple-element.20.k, ...), custom_call_target="tpu_custom_call" | custom-call | flops 20000000000 | bytes 10000000 | tf_op jit(solution)/shard_map/attend1/pallas_call | solution.py:262
  144.3 12.0 %psum.7.sums = f32[8,128]{1,0:T(8,128)} all-reduce(f32[8,128]{1,0:T(8,128)} %get-tuple-element.27), channel_id=1, replica_groups=mesh['dp'=8,'sp'=16] {'dp'}, use_global_device_ids=true, to_apply=%region_2.3 | all-reduce | flops 1024 | bytes 8192 | tf_op jit(solution)/shard_map/psum | solution.py:446
  156.3 1.5 sums.1
  157.9 0.0 all-to-all-done.3.recv
  157.9 0.0 copy-start.1
  157.9 1.3 copy-done.1
  159.2 6.9 %all-to-all-start.2 = ((bf16[16,136,768]{2,1,0:T(8,128)(2,1)}), bf16[16,136,768]{2,1,0:T(8,128)(2,1)S(1)}, u32[]{:S(2)}, u32[]{:S(2)}) async-start(bf16[16,136,768]{2,1,0:T(8,128)(2,1)} %sums.1), calls=%async_computation.2 | async-start | bytes 6684672 | tf_op jit(solution)/shard_map/all_to_all | solution.py:409
  166.2 3.2 %unpack0.1 = (bf16[128,8192]{1,0:T(8,128)(2,1)}, bf16[128,8192]{1,0:T(8,128)(2,1)}) custom-call(bf16[16,128,512]{2,1,0:T(8,128)(2,1)} %copy-done.1), custom_call_target="tpu_custom_call" | custom-call | bytes 4194304 | tf_op jit(solution)/shard_map/unpack0/pallas_call | solution.py:328
  169.3 48.9 %all-to-all-done.2.recv = bf16[16,136,768]{2,1,0:T(8,128)(2,1)S(1)} async-done(((bf16[16,136,768]{2,1,0:T(8,128)(2,1)}), bf16[16,136,768]{2,1,0:T(8,128)(2,1)S(1)}, u32[]{:S(2)}, u32[]{:S(2)}) %all-to-all-start.2) | async-done | bytes 3342368 | tf_op jit(solution)/shard_map/all_to_all | solution.py:409
  218.3 0.0 copy-start
  218.3 1.7 copy-done
  220.0 4.3 %unpack1.1 = (bf16[128,8192]{1,0:T(8,128)(2,1)}, bf16[128,8192]{1,0:T(8,128)(2,1)}, bf16[128,2048]{1,0:T(8,128)(2,1)}, f32[1,10240]{1,0:T(1,128)}) custom-call(bf16[16,136,768]{2,1,0:T(8,128)(2,1)} %copy-done, bf16[128,8192]{1,0:T(8,128)(2,1)} %get-tuple-element.30._a, ...), custom_call_target="tpu_custom_call", output_to_operand_aliasing={{0}: (1, {}), {1}: (2, {})} | custom-call | bytes 6291456 | tf_op jit(solution)/shard_map/unpack1/pallas_call | solution.py:381
  (4 shorter events, 0.0 us)
Async XLA Ops:
  4.8 54.7 %all-to-all-start.1 = ((bf16[16,128,768]{2,1,0:T(8,128)(2,1)}), bf16[16,128,768]{2,1,0:T(8,128)(2,1)S(1)}, u32[]{:S(2)}, u32[]{:S(2)}) async-start(bf16[16,128,768]{2,1,0:T(8,128)(2,1)} %pack0.1), calls=%async_computation.1 | async-start | bytes 6291456 | tf_op jit(solution)/shard_map/all_to_all | solution.py:409
  11.8 3.2 %copy-start.4 = (s32[1,4]{1,0:T(1,128)S(1)}, s32[1,4]{1,0:T(1,128)}, u32[]{:S(2)}) copy-start(s32[1,4]{1,0:T(1,128)} %param.8) | copy-start | bytes 52
  15.3 44.1 %copy-start.3 = (s32[2048]{0:T(1024)}, s32[2048]{0:T(1024)S(1)}, u32[]{:S(2)}) copy-start(s32[2048]{0:T(1024)S(1)} %select_reduce_fusion) | copy-start | bytes 24580
  59.5 4.5 %copy-start.2 = (bf16[16,128,768]{2,1,0:T(8,128)(2,1)}, bf16[16,128,768]{2,1,0:T(8,128)(2,1)S(1)}, u32[]{:S(2)}) copy-start(bf16[16,128,768]{2,1,0:T(8,128)(2,1)S(1)} %all-to-all-done.1) | copy-start | bytes 9437188
  59.5 43.3 %all-to-all-start = ((bf16[16,128,512]{2,1,0:T(8,128)(2,1)}), bf16[16,128,512]{2,1,0:T(8,128)(2,1)}, u32[]{:S(2)}, u32[]{:S(2)}) async-start(bf16[16,128,512]{2,1,0:T(8,128)(2,1)} %pack1.1), calls=%async_computation | async-start | bytes 4194304 | tf_op jit(solution)/shard_map/all_to_all | solution.py:409
  102.7 55.1 %all-to-all-start.3 = ((bf16[16,128,512]{2,1,0:T(8,128)(2,1)}), bf16[16,128,512]{2,1,0:T(8,128)(2,1)S(1)}, u32[]{:S(2)}, u32[]{:S(2)}) async-start(bf16[16,128,512]{2,1,0:T(8,128)(2,1)} %get-tuple-element.29), calls=%async_computation.3 | async-start | bytes 4194304 | tf_op jit(solution)/shard_map/all_to_all | solution.py:409
  157.9 1.4 copy-start.1
  159.2 59.0 %all-to-all-start.2 = ((bf16[16,136,768]{2,1,0:T(8,128)(2,1)}), bf16[16,136,768]{2,1,0:T(8,128)(2,1)S(1)}, u32[]{:S(2)}, u32[]{:S(2)}) async-start(bf16[16,136,768]{2,1,0:T(8,128)(2,1)} %sums.1), calls=%async_computation.2 | async-start | bytes 6684672 | tf_op jit(solution)/shard_map/all_to_all | solution.py:409
  218.3 1.7 copy-start

commit v2 on v1

v2 whole, which is shorter than its diff:
```python
import functools

import jax
import jax.numpy as jnp
from jax import lax
from jax.experimental import pallas as pl
from jax.experimental.pallas import tpu as pltpu
from jax.sharding import PartitionSpec as P

QUERY_HEADS = 64
KEY_VALUE_HEADS = 8
HEAD = 128
PAGE = 16
BLK = 256
SCALE = HEAD ** (-0.5)
LOG2E = 1.4426950408889634
NEG = -1e30
ROPE_BASE = 1000000.0

BF = jnp.bfloat16
F32 = jnp.float32
ANY = pl.BlockSpec(memory_space=pl.ANY)
VM = pl.BlockSpec(memory_space=pltpu.VMEM)
SM = pl.BlockSpec(memory_space=pltpu.SMEM)


def params(mib):
    return pltpu.CompilerParams(vmem_limit_bytes=mib * 1024 * 1024)


def cost(flops, nbytes):
    return pl.CostEstimate(flops=flops, bytes_accessed=nbytes, transcendentals=0)


def pack_kernel(chunk, ways, proj, cot, out, buf, sem, out_sem):
    kv0 = QUERY_HEADS * HEAD
    copies_of = ways // KEY_VALUE_HEADS
    fetch = []
    for d in range(ways):
        col = d * 512 + chunk * 256
        moves = [
            (proj.at[:, pl.ds(col, 256)], buf.at[d, :, pl.ds(0, 256)]),
            (cot.at[:, pl.ds(col, 256)], buf.at[d, :, pl.ds(256, 256)]),
        ]
        if chunk == 0:
            kcol = kv0 + (d // copies_of) * HEAD
            vcol = kcol + KEY_VALUE_HEADS * HEAD
            moves.append((proj.at[:, pl.ds(kcol, HEAD)], buf.at[d, :, pl.ds(512, HEAD)]))
            moves.append((proj.at[:, pl.ds(vcol, HEAD)], buf.at[d, :, pl.ds(640, HEAD)]))
        fetch.append([pltpu.make_async_copy(x, y, sem.at[d, m]) for m, (x, y) in enumerate(moves)])
    for group in fetch:
        for copy in group:
            copy.start()
    stores = []
    for d in range(ways):
        for copy in fetch[d]:
            copy.wait()
        stores.append(pltpu.make_async_copy(buf.at[d], out.at[d], out_sem.at[d]))
        stores[-1].start()
    for copy in stores:
        copy.wait()


def pack(chunk, ways, proj, cot):
    rows = proj.shape[0]
    width = 768 if chunk == 0 else 512
    return pl.pallas_call(
        functools.partial(pack_kernel, chunk, ways),
        out_shape=jax.ShapeDtypeStruct((ways, rows, width), BF),
        in_specs=[ANY, ANY],
        out_specs=ANY,
        scratch_shapes=[
            pltpu.VMEM((ways, rows, width), BF),
            pltpu.SemaphoreType.DMA((ways, 4)),
            pltpu.SemaphoreType.DMA((ways,)),
        ],
        compiler_params=params(8),
        cost_estimate=cost(0, 4 * ways * rows * width),
        name=f"pack{chunk}",
    )(proj, cot)


def rope(x, c, s):
    return x * c + pltpu.roll(x, HEAD // 2, 1) * s


def unrope(g, c, s):
    return g * c - pltpu.roll(g, HEAD // 2, 1) * s


def attend_kernel(last, *refs):
    if last:
        (first_block, page, recv, k, v, kt, vt, cos, sin, first, bias, dk_in, dv_in, sums_in,
         out, dk, dv, sums, q_raw, do_raw, st, ot, dqt, sem) = refs
    else:
        (first_block, page, recv, cos, sin, first, bias,
         out, k, v, kt, vt, dk, dv, sums, kv_raw, q_raw, do_raw, st, ot, dqt, sem) = refs
    n = recv.shape[0]
    blocks = n // BLK
    per = BLK // 128

    upstream = pltpu.make_async_copy(recv.at[:, pl.ds(256, 256)], do_raw, sem.at[0])
    upstream.start()

    def fetch(p, _):
        src = pl.ds(pl.multiple_of(page[p] * PAGE, PAGE), PAGE)
        dst = pl.ds(pl.multiple_of(p * PAGE, PAGE), PAGE)
        if not last:
            pltpu.make_async_copy(recv.at[src, pl.ds(512, 256)], kv_raw.at[dst, :], sem.at[2]).start()
        pltpu.make_async_copy(recv.at[src, pl.ds(0, 256)], q_raw.at[dst, :], sem.at[1]).start()
        return 0

    lax.fori_loop(0, n // PAGE, fetch, 0, unroll=4)
    if last:
        dk[...] = dk_in[...]
        dv[...] = dv_in[...]
    else:
        dk[...] = jnp.zeros_like(dk)
        dv[...] = jnp.zeros_like(dv)
        pltpu.make_async_copy(recv.at[:, pl.ds(512, 256)], kv_raw, sem.at[2]).wait()

        def prepare(b, _):
            rows = pl.ds(pl.multiple_of(b * BLK, BLK), BLK)
            x = rope(kv_raw[rows, 0:HEAD].astype(F32) + bias[2:3, :], cos[rows, :], sin[rows, :])
            y = kv_raw[rows, HEAD : 2 * HEAD].astype(F32) + bias[3:4, :]
            k[rows, :] = x.astype(BF)
            v[rows, :] = y.astype(BF)
            kt[:, rows] = jnp.transpose(x).astype(BF)
            vt[:, rows] = jnp.transpose(y).astype(BF)
            return 0

        lax.fori_loop(0, blocks, prepare, 0)
    pltpu.make_async_copy(recv.at[:, pl.ds(0, 256)], q_raw, sem.at[1]).wait()
    upstream.wait()

    nt = (((1,), (1,)), ((), ()))
    nn = (((1,), (0,)), ((), ()))

    def block(i, carry):
        rows = pl.ds(pl.multiple_of(i * BLK, BLK), BLK)
        c, s = cos[rows, :], sin[rows, :]
        q = jnp.concatenate(
            [
                rope(q_raw[rows, h * HEAD : (h + 1) * HEAD].astype(F32) + bias[h : h + 1, :], c, s).astype(BF)
                for h in range(2)
            ],
            0,
        )
        do = jnp.concatenate([do_raw[rows, 0:128], do_raw[rows, 128:256]], 0)
        lo = first_block[i]
        start1 = first[0:1, rows]
        start = jnp.concatenate([start1, start1], 1)
        lane = lax.broadcasted_iota(jnp.int32, (1, BLK), 1) + i * BLK
        token = jnp.concatenate([lane, lane], 1)

        def score(j, m):
            cols = pl.ds(pl.multiple_of(j * BLK, BLK), BLK)
            s = lax.dot_general(k[cols, :], q, nt, preferred_element_type=F32) * (SCALE * LOG2E)
            key = lax.broadcasted_iota(jnp.int32, (BLK, 2 * BLK), 0)
            s = jnp.where((key <= token - j * BLK) & (key >= start - j * BLK), s, NEG)
            st[j - lo] = s
            return jnp.maximum(m, jnp.max(s, 0, keepdims=True))

        m = lax.fori_loop(lo, i + 1, score, jnp.full((1, 2 * BLK), NEG, F32))
        ot[...] = jnp.zeros_like(ot)

        def value(j, total):
            cols = pl.ds(pl.multiple_of(j * BLK, BLK), BLK)
            e = jnp.exp2(st[j - lo] - m)
            st[j - lo] = e
            ot[...] += lax.dot_general(vt[:, cols], e.astype(BF), nn, preferred_element_type=F32)
            return total + jnp.sum(e, 0, keepdims=True)

        total = lax.fori_loop(lo, i + 1, value, jnp.zeros((1, 2 * BLK), F32))
        inv = 1.0 / total
        o_t = (ot[...] * inv).astype(BF).astype(F32)
        do_t = jnp.transpose(do.astype(F32))
        delta = jnp.sum(o_t * do_t, 0, keepdims=True)
        dqt[...] = jnp.zeros_like(dqt)

        def back(j, _):
            cols = pl.ds(pl.multiple_of(j * BLK, BLK), BLK)
            p = st[j - lo] * inv
            dp = lax.dot_general(v[cols, :], do, nt, preferred_element_type=F32)
            ds = (p * (dp - delta)).astype(BF)
            dv[cols, :] += lax.dot_general(p.astype(BF), do, nn, preferred_element_type=F32)
            dk[cols, :] += lax.dot_general(ds, q, nn, preferred_element_type=F32)
            dqt[...] += lax.dot_general(kt[:, cols], ds, nn, preferred_element_type=F32)
            return 0

        lax.fori_loop(lo, i + 1, back, 0)
        o = jnp.transpose(o_t).astype(BF)
        dq = jnp.transpose(dqt[...]) * SCALE
        new = []
        for h in range(2):
            g = unrope(dq[h * BLK : (h + 1) * BLK], c, s).astype(BF)
            new.append(carry[h] + jnp.sum(g.astype(F32), 0, keepdims=True))
            for a in range(per):
                part = slice(a * 128, (a + 1) * 128)
                out[i * per + a, :, h * HEAD : (h + 1) * HEAD] = o[h * BLK + a * 128 : h * BLK + (a + 1) * 128]
                out[i * per + a, :, 256 + h * HEAD : 256 + (h + 1) * HEAD] = g[part]
        return tuple(new)

    zero = jnp.zeros((1, HEAD), F32)
    head_sums = lax.fori_loop(0, blocks, block, (zero, zero))
    if not last:
        sums[...] = jnp.zeros_like(sums)
        sums[0:1, :] = head_sums[0]
        sums[1:2, :] = head_sums[1]
        return

    def finish(b, carry):
        rows = pl.ds(pl.multiple_of(b * 128, 128), 128)
        gk = unrope(dk[rows, :] * SCALE, cos[rows, :], sin[rows, :])
        gv = dv[rows, :]
        out[b, :, 512:640] = gk.astype(BF)
        out[b, :, 640:768] = gv.astype(BF)
        return (
            carry[0] + jnp.sum(gk, 0, keepdims=True),
            carry[1] + jnp.sum(gv, 0, keepdims=True),
        )

    kv_sums = lax.fori_loop(0, n // 128, finish, (zero, zero))
    sums[...] = sums_in[...]
    sums[2:3, :] = head_sums[0]
    sums[3:4, :] = head_sums[1]
    sums[4:5, :] = kv_sums[0]
    sums[5:6, :] = kv_sums[1]


def attend(last, ways, first_block, page, recv, cos, sin, first, bias, keys=(), state=()):
    n = recv.shape[0]
    grad = jax.ShapeDtypeStruct((n, HEAD), F32)
    row = jax.ShapeDtypeStruct((n, HEAD), BF)
    col = jax.ShapeDtypeStruct((HEAD, n), BF)
    sums = jax.ShapeDtypeStruct((8, HEAD), F32)
    out = jax.ShapeDtypeStruct((ways, n // ways, 768 if last else 512), BF)
    if last:
        args = (first_block, page, recv, *keys, cos, sin, first, bias, *state)
        outs = (out, sums)
        scratch = [pltpu.VMEM((n, HEAD), F32), pltpu.VMEM((n, HEAD), F32)]
    else:
        args = (first_block, page, recv, cos, sin, first, bias)
        outs = (out, row, row, col, col, grad, grad, sums)
        scratch = [pltpu.VMEM((n, 256), BF)]

    def body(*refs):
        if last:
            head, tail = refs[: len(args)], refs[len(args) :]
            o, sm, gk, gv = tail[:4]
            refs = (*head, o, gk, gv, sm, *tail[4:])
        attend_kernel(last, *refs)

    return pl.pallas_call(
        body,
        out_shape=outs,
        in_specs=[SM, SM, ANY] + [VM] * (len(args) - 3),
        out_specs=tuple([VM] * len(outs)),
        scratch_shapes=scratch
        + [
            pltpu.VMEM((n, 256), BF),
            pltpu.VMEM((n, 256), BF),
            pltpu.VMEM((1024 // BLK + 1, BLK, 2 * BLK), F32),
            pltpu.VMEM((HEAD, 2 * BLK), F32),
            pltpu.VMEM((HEAD, 2 * BLK), F32),
            pltpu.SemaphoreType.DMA((3,)),
        ],
        compiler_params=params(32),
        cost_estimate=cost(20 * 10**9, 10**7),
        name="attend1" if last else "attend0",
    )(*args)


def unpack_heads(recv, buf, att, gq, chunk, sem, out_sem):
    ways = buf.shape[0]
    fetch = [pltpu.make_async_copy(recv.at[d], buf.at[d], sem.at[d]) for d in range(ways)]
    for copy in fetch:
        copy.start()
    stores = []
    for d in range(ways):
        cols = pl.ds(d * 512 + chunk * 256, 256)
        fetch[d].wait()
        stores.append(pltpu.make_async_copy(buf.at[d, :, pl.ds(0, 256)], att.at[:, cols], out_sem.at[d, 0]))
        stores.append(pltpu.make_async_copy(buf.at[d, :, pl.ds(256, 256)], gq.at[:, cols], out_sem.at[d, 1]))
        stores[-2].start()
        stores[-1].start()
    return stores


def unpack0_kernel(recv, att, gq, buf, sem, out_sem):
    for copy in unpack_heads(recv, buf, att, gq, 0, sem, out_sem):
        copy.wait()


def unpack_scratch(recv):
    ways = recv.shape[0]
    return [
        pltpu.VMEM(recv.shape, BF),
        pltpu.SemaphoreType.DMA((ways,)),
        pltpu.SemaphoreType.DMA((ways, 2)),
    ]


def unpack0(recv):
    ways, rows, _ = recv.shape
    shape = jax.ShapeDtypeStruct((rows, QUERY_HEADS * HEAD), BF)
    return pl.pallas_call(
        unpack0_kernel,
        out_shape=(shape, shape),
        in_specs=[ANY],
        out_specs=(ANY, ANY),
        scratch_shapes=unpack_scratch(recv),
        compiler_params=params(8),
        cost_estimate=cost(0, 4 * ways * rows * 512),
        name="unpack0",
    )(recv)


def unpack1_kernel(recv, _a, _g, att, gq, kvg, buf, sem, out_sem):
    ways = buf.shape[0]
    stores = unpack_heads(recv, buf, att, gq, 1, sem, out_sem)
    share = ways // KEY_VALUE_HEADS
    kw = KEY_VALUE_HEADS * HEAD
    for h in range(KEY_VALUE_HEADS):
        grad = buf[h * share, :, 512:768].astype(F32)
        for r in range(1, share):
            grad = grad + buf[h * share + r, :, 512:768].astype(F32)
        kvg[:, h * HEAD : (h + 1) * HEAD] = grad[:, :HEAD].astype(BF)
        kvg[:, kw + h * HEAD : kw + (h + 1) * HEAD] = grad[:, HEAD:].astype(BF)
    for copy in stores:
        copy.wait()


def unpack1(recv, att, gq):
    ways = recv.shape[0]
    rows = att.shape[0]
    return pl.pallas_call(
        unpack1_kernel,
        out_shape=(
            jax.ShapeDtypeStruct(att.shape, BF),
            jax.ShapeDtypeStruct(gq.shape, BF),
            jax.ShapeDtypeStruct((rows, 2 * KEY_VALUE_HEADS * HEAD), BF),
        ),
        in_specs=[ANY, ANY, ANY],
        out_specs=(ANY, ANY, VM),
        input_output_aliases={1: 0, 2: 1},
        scratch_shapes=unpack_scratch(recv),
        compiler_params=params(8),
        cost_estimate=cost(0, 4 * ways * rows * 768),
        name="unpack1",
    )(recv, att, gq)


def rope_tables(positions):
    lane = jnp.arange(HEAD, dtype=jnp.int32)
    exponent = (lane % (HEAD // 2)).astype(F32) * 2.0 / HEAD
    frequency = jnp.power(jnp.float32(ROPE_BASE), -exponent)
    angles = positions.astype(F32)[:, None] * frequency[None, :]
    sign = jnp.where(lane < HEAD // 2, -1.0, 1.0).astype(F32)
    return jnp.cos(angles), jnp.sin(angles) * sign[None, :]


def exchange(x):
    return lax.all_to_all(x, "sp", split_axis=0, concat_axis=0, tiled=True)


def shards(projected, bias, cotangent, lengths, page_source):
    ways = lax.axis_size("sp")
    me = lax.axis_index("sp")
    rows = projected.shape[0]
    n = rows * ways
    page = page_source[0]
    recv0 = exchange(pack(0, ways, projected, cotangent))
    recv1 = exchange(pack(1, ways, projected, cotangent))

    ends = jnp.cumsum(lengths[0])
    starts = ends - lengths[0]
    tokens = jnp.arange(n, dtype=jnp.int32)
    first = jnp.max(jnp.where(tokens[:, None] >= starts[None, :], starts[None, :], 0), 1)
    first_block = first.reshape(n // BLK, BLK)[:, 0] // BLK
    cos, sin = rope_tables(tokens - first)
    first = first[None, :]

    share = ways // KEY_VALUE_HEADS
    kv_head = me // share
    bias_rows = bias.reshape(-1, HEAD)
    qbias = lax.dynamic_slice_in_dim(bias_rows, me * 4, 4)
    kbias = lax.dynamic_slice_in_dim(bias_rows, QUERY_HEADS + kv_head, 1)
    vbias = lax.dynamic_slice_in_dim(bias_rows, QUERY_HEADS + KEY_VALUE_HEADS + kv_head, 1)
    bias0 = jnp.concatenate([qbias[0:2], kbias, vbias], 0)

    send2, k, v, kt, vt, dk, dv, sums = attend(
        False, ways, first_block, page, recv0.reshape(n, 768), cos, sin, first, bias0
    )
    recv2 = exchange(send2)
    send3, sums = attend(
        True, ways, first_block, page, recv1.reshape(n, 512), cos, sin, first, qbias[2:4],
        (k, v, kt, vt), (dk, dv, sums),
    )
    recv3 = exchange(send3)
    sums = lax.all_gather(lax.psum(sums, "dp"), "sp")
    att, gq = unpack0(recv2)
    att, gq, kvg = unpack1(recv3, att, gq)
    kv_sums = jnp.sum(sums[:, 4:6].reshape(KEY_VALUE_HEADS, share, 2, HEAD), 1)
    gb = jnp.concatenate(
        [sums[:, 0:4].reshape(-1), kv_sums[:, 0].reshape(-1), kv_sums[:, 1].reshape(-1)]
    )
    return att, gq, kvg, gb


def solution(mesh):
    in_specs = (P(("dp", "sp"), None), P(), P(("dp", "sp"), None), P("dp", None), P("dp", None))
    out_specs = (P(("dp", "sp"), None), P(("dp", "sp"), None), P(("dp", "sp"), None), P())
    return jax.shard_map(shards, mesh=mesh, in_specs=in_specs, out_specs=out_specs, check_vma=False)
```

time: 226 us -> 226 us (level); the launches traced: 224 us -> 230 us
  waiting for transfers between devices: 84.2 us -> 36.9 us
  blocking collectives: 12 us -> 54.5 us
  local copies, waits for them, and re-layouts: 5.72 us -> 29.5 us
  Pallas kernels: 88.9 us -> 75.9 us
    all_to_all x4, waiting for transfers between devices: 84.2 us -> 36.9 us  [exchange(): return lax.all_to_all(x, 'sp', split_axis=0, concat_axis=0, tiled=True)]
    all_gather x0 -> x1, blocking collectives: none -> 43.9 us  [shards(): sums = lax.all_gather(lax.psum(sums, 'dp'), 'sp')]
    unnamed x10 -> x52, local copies, waits for them, and re-layouts: 3.07 us -> 27.9 us
    pallas_call x5 -> x3, Pallas kernels: 77.3 us -> 64 us  [the longest x2 59.6 us: attend(): pl.pallas_call(body, out_shape=outs, in_specs=[SM, SM, ANY] + [VM] * (len...]
  transfers between devices with their start and end apart: 4 -> 4, of which waited for: 2 -> 1; matrix products, arithmetic and copies ran while one was open for 4% -> 3% of each run, Pallas kernels for 36% -> 29%
where the time goes in v2:
time: 226 us; the launch traced here: 230 us
  Pallas kernels  75.9 us (34%)
  blocking collectives  54.5 us (24%)
  waiting for transfers between devices  36.9 us (16%)
  local copies, waits for them, and re-layouts  29.5 us (13%)
  starting transfers between devices  26 us (12%)
  other arithmetic  5.94 us (3%)
    pallas_call x2, Pallas kernels, attend(): pl.pallas_call(body, out_shape=outs, in_specs=[SM, SM, ANY] + [VM] * (len...  59.6 us
    all_gather x1, blocking collectives, shards(): sums = lax.all_gather(lax.psum(sums, 'dp'), 'sp')  43.9 us
    all_to_all x4, waiting for transfers between devices, exchange(): return lax.all_to_all(x, 'sp', split_axis=0, concat_axis=0, tiled=True)  36.9 us
    unnamed x52, local copies, waits for them, and re-layouts  27.9 us
    all_to_all x4, starting transfers between devices, exchange(): return lax.all_to_all(x, 'sp', split_axis=0, concat_axis=0, tiled=True)  26 us
    psum x1, blocking collectives, shards(): sums = lax.all_gather(lax.psum(sums, 'dp'), 'sp')  10.6 us
    pallas_call x1, Pallas kernels, unpack1(): pl.pallas_call(unpack1_kernel, out_shape=(jax.ShapeDtypeStruct(att.shape,...  6.56 us
    pallas_call x2, Pallas kernels, pack(): pl.pallas_call(functools.partial(pack_kernel, chunk, ways), out_shape=jax...  5.31 us
  transfers between devices with their start and end apart: 4, of which 1 were waited for; matrix products, arithmetic and copies ran while one was open for 3% of the time, Pallas kernels for 29%

profile of v2, /device:TPU:64, one launch (start us, length us, event | category | flops | bytes accessed | tf_op | source)
XLA Modules:
  0.0 229.5 jit_solution(12908364252328328144)
XLA Ops:
  0.6 0.0 copy-start
  0.6 1.7 copy-done
  2.4 1.6 copy-done.4
  4.0 3.0 %pack0.1 = bf16[16,128,768]{2,1,0:T(8,128)(2,1)} custom-call(bf16[128,10240]{1,0:T(8,128)(2,1)S(1)} %copy-done, bf16[128,8192]{1,0:T(8,128)(2,1)S(1)} %copy-done.4), custom_call_target="tpu_custom_call" | custom-call | bytes 6291456 | tf_op jit(solution)/shard_map/pack0/pallas_call | solution.py:67
  7.0 0.0 copy-start.1
  7.0 7.2 %all-to-all-start.1 = ((bf16[16,128,768]{2,1,0:T(8,128)(2,1)}), bf16[16,128,768]{2,1,0:T(8,128)(2,1)}, u32[]{:S(2)}, u32[]{:S(2)}) async-start(bf16[16,128,768]{2,1,0:T(8,128)(2,1)} %pack0.1), calls=%async_computation.1 | async-start | bytes 6291456 | tf_op jit(solution)/shard_map/all_to_all | solution.py:364
  14.2 0.0 copy-done.1
  14.2 0.0 copy-start.5
  14.2 1.6 copy-done.5
  15.8 0.0 copy-start.25
  15.8 2.3 %pack1.1 = bf16[16,128,512]{2,1,0:T(8,128)(2,1)} custom-call(bf16[128,10240]{1,0:T(8,128)(2,1)S(1)} %copy-done.1, bf16[128,8192]{1,0:T(8,128)(2,1)S(1)} %copy-done.5), custom_call_target="tpu_custom_call" | custom-call | bytes 4194304 | tf_op jit(solution)/shard_map/pack1/pallas_call | solution.py:67
  18.2 0.0 copy-done.25
  18.2 0.2 reduce-window_clone.1
  18.4 0.1 select_reduce_fusion
  18.5 0.7 constant_dynamic-slice_fusion.1
  19.2 0.7 constant_dynamic-slice_fusion.2
  19.9 0.1 slice_reduce_fusion
  20.1 5.0 %fusion = (f32[2048,128]{1,0:T(8,128)S(1)}, f32[2048,128]{1,0:T(8,128)}) fusion(f32[128]{0:T(128)S(1)} %get-tuple-element.42, f32[128]{0:T(128)S(1)} %get-tuple-element.43, f32[2048]{0:T(1024)S(1)} %subtract_convert_fusion), kind=kLoop, calls=%fused_computation.2 | loop fusion | flops 524288 | bytes 2106368 | tf_op jit(solution)/shard_map/mul | solution.py:360
  25.0 0.0 copy-start.12
  25.0 36.9 %all-to-all-done.1 = bf16[16,128,768]{2,1,0:T(8,128)(2,1)} async-done(((bf16[16,128,768]{2,1,0:T(8,128)(2,1)}), bf16[16,128,768]{2,1,0:T(8,128)(2,1)}, u32[]{:S(2)}, u32[]{:S(2)}) %all-to-all-start.1) | async-done | bytes 3145760 | tf_op jit(solution)/shard_map/all_to_all | solution.py:364
  61.9 4.3 %all-to-all-start = ((bf16[16,128,512]{2,1,0:T(8,128)(2,1)}), bf16[16,128,512]{2,1,0:T(8,128)(2,1)S(1)}, u32[]{:S(2)}, u32[]{:S(2)}) async-start(bf16[16,128,512]{2,1,0:T(8,128)(2,1)} %pack1.1), calls=%async_computation | async-start | bytes 4194304 | tf_op jit(solution)/shard_map/all_to_all | solution.py:364
  66.3 0.0 copy-done.12
  66.3 0.0 copy-start.10
  66.3 1.2 copy-done.10
  67.5 30.1 %attend0.1 = (bf16[16,128,512]{2,1,0:T(8,128)(2,1)S(1)}, bf16[2048,128]{1,0:T(8,128)(2,1)S(1)}, bf16[2048,128]{1,0:T(8,128)(2,1)S(1)}, bf16[128,2048]{1,0:T(8,12...) custom-call(s32[8]{0:T(128)S(1)} %and_select_fusion.1.refs_0_, ...), custom_call_target="tpu_custom_call" | custom-call | flops 20000000000 | bytes 10000000 | tf_op jit(solution)/shard_map/attend0/pallas_call | solution.py:254
  97.6 0.0 copy-start.9
  97.7 1.3 copy-done.9
  99.0 0.0 copy-start.13
  99.0 1.0 copy-done.13
  100.0 0.0 copy-start.15
  100.0 1.0 copy-done.15
  100.9 0.0 copy-start.17
  100.9 0.8 copy-done.17
  101.7 0.0 copy-start.19
  101.7 0.8 copy-done.19
  102.5 0.0 copy-start.21
  102.5 0.8 copy-done.21
  103.3 0.0 copy-start.23
  103.4 0.8 copy-done.23
  104.2 0.0 all-to-all-done
  104.2 1.3 copy-done.7
  105.5 7.2 %all-to-all-start.3 = ((bf16[16,128,512]{2,1,0:T(8,128)(2,1)}), bf16[16,128,512]{2,1,0:T(8,128)(2,1)S(1)}, u32[]{:S(2)}, u32[]{:S(2)}) async-start(bf16[16,128,512]{2,1,0:T(8,128)(2,1)} %copy-done.9), calls=%async_computation.3 | async-start | bytes 4194304 | tf_op jit(solution)/shard_map/all_to_all | solution.py:364
  112.7 0.0 copy-start.8
  112.7 1.6 copy-done.8
  114.3 1.2 copy-done.11
  115.5 1.2 copy-done.14
  116.7 1.2 copy-done.16
  118.0 1.0 copy-done.18
  119.0 1.0 copy-done.20
  120.1 1.0 copy-done.22
  121.1 1.0 copy-done.24
  122.1 29.5 %attend1.1 = (bf16[16,128,768]{2,1,0:T(8,128)(2,1)S(1)}, f32[8,128]{1,0:T(8,128)S(1)}) custom-call(s32[8]{0:T(128)S(1)} %and_select_fusion.1.refs_0_, s32[128]{0:T(128)S(1)} %bitcast.18, bf16[2048,512]{1,0:T(8,128)(2,1)S(1)} %bitcast.13, bf16[2048,128]{1,0:T(8,128)(2,1)S(1)} %copy-done.18, bf16[2048,128]{1,0:T(8,128)(2,1)S(1)} %copy-done.20, ...), custom_call_target="tpu_custom_call" | custom-call | flops 20000000000 | bytes 10000000 | tf_op jit(solution)/shard_map/attend1/pallas_call | solution.py:254
  151.6 0.0 copy-start.6
  151.7 1.6 copy-done.6
  153.3 0.0 all-to-all-done.3.recv
  153.3 1.3 copy-done.2
  154.6 7.2 %all-to-all-start.2 = ((bf16[16,128,768]{2,1,0:T(8,128)(2,1)}), bf16[16,128,768]{2,1,0:T(8,128)(2,1)S(1)}, u32[]{:S(2)}, u32[]{:S(2)}) async-start(bf16[16,128,768]{2,1,0:T(8,128)(2,1)} %copy-done.6), calls=%async_computation.2 | async-start | bytes 6291456 | tf_op jit(solution)/shard_map/all_to_all | solution.py:364
  161.8 10.6 %psum.7 = f32[1,8,128]{2,1,0:T(8,128)S(1)} all-reduce(f32[1,8,128]{2,1,0:T(8,128)S(1)} %bitcast.16), channel_id=1, replica_groups=mesh['dp'=8,'sp'=16] {'dp'}, use_global_device_ids=true, to_apply=%region_2.3 | all-reduce | flops 1024 | bytes 8192 | tf_op jit(solution)/shard_map/psum | solution.py:401
  172.4 43.9 %all_gather.7 = f32[16,8,128]{2,1,0:T(8,128)S(1)} all-gather(f32[1,8,128]{2,1,0:T(8,128)S(1)} %psum.7), channel_id=1, replica_groups=mesh['dp'=8,'sp'=16] {'sp'}, dimensions={0}, use_global_device_ids=true | all-gather | bytes 69632 | tf_op jit(solution)/shard_map/all_gather | solution.py:401
  216.4 0.6 pad_maximum_fusion
  217.0 1.6 copy-done.3
  218.6 4.4 %unpack0.1 = (bf16[128,8192]{1,0:T(8,128)(2,1)}, bf16[128,8192]{1,0:T(8,128)(2,1)}) custom-call(bf16[16,128,512]{2,1,0:T(8,128)(2,1)S(1)} %copy-done.3), custom_call_target="tpu_custom_call" | custom-call | bytes 4194304 | tf_op jit(solution)/shard_map/unpack0/pallas_call | solution.py:307
  223.0 0.0 all-to-all-done.2.recv
  223.0 6.6 %unpack1.1 = (bf16[128,8192]{1,0:T(8,128)(2,1)}, bf16[128,8192]{1,0:T(8,128)(2,1)}, bf16[128,2048]{1,0:T(8,128)(2,1)}) custom-call(bf16[16,128,768]{2,1,0:T(8,128)(2,1)S(1)} %all-to-all-done.2.recv, bf16[128,8192]{1,0:T(8,128)(2,1)} %get-tuple-element.28._a, bf16[128,8192]{1,0:T(8,128)(2,1)} %get-tuple-element.29._g), custom_call_target="tpu_custom_call", output_to_operand_aliasing={{0}: (1, {}), {1}: (2, {})} | custom-call | bytes 6291456 | tf_op jit(solution)/shard_map/unpack1/pallas_call | solution.py:337
  (21 shorter events, 0.1 us)
Async XLA Ops:
  0.6 1.7 copy-start
  2.4 1.6 copy-start.4
  7.0 7.3 %copy-start.1 = (bf16[128,10240]{1,0:T(8,128)(2,1)S(1)}, bf16[128,10240]{1,0:T(8,128)(2,1)}, u32[]{:S(2)}) copy-start(bf16[128,10240]{1,0:T(8,128)(2,1)} %proj.3) | copy-start | bytes 7864324
  7.0 54.9 %all-to-all-start.1 = ((bf16[16,128,768]{2,1,0:T(8,128)(2,1)}), bf16[16,128,768]{2,1,0:T(8,128)(2,1)}, u32[]{:S(2)}, u32[]{:S(2)}) async-start(bf16[16,128,768]{2,1,0:T(8,128)(2,1)} %pack0.1), calls=%async_computation.1 | async-start | bytes 6291456 | tf_op jit(solution)/shard_map/all_to_all | solution.py:364
  14.2 1.6 copy-start.5
  15.8 2.4 %copy-start.25 = (s32[1,4]{1,0:T(1,128)S(1)}, s32[1,4]{1,0:T(1,128)}, u32[]{:S(2)}) copy-start(s32[1,4]{1,0:T(1,128)} %param.8) | copy-start | bytes 52
  25.0 41.2 %copy-start.12 = (s32[1,128]{1,0:T(1,128)S(1)}, s32[1,128]{1,0:T(1,128)}, u32[]{:S(2)}) copy-start(s32[1,128]{1,0:T(1,128)} %param.9) | copy-start | bytes 1540
  61.9 42.2 %all-to-all-start = ((bf16[16,128,512]{2,1,0:T(8,128)(2,1)}), bf16[16,128,512]{2,1,0:T(8,128)(2,1)S(1)}, u32[]{:S(2)}, u32[]{:S(2)}) async-start(bf16[16,128,512]{2,1,0:T(8,128)(2,1)} %pack1.1), calls=%async_computation | async-start | bytes 4194304 | tf_op jit(solution)/shard_map/all_to_all | solution.py:364
  66.3 1.2 copy-start.10
  97.6 1.3 copy-start.9
  99.0 1.0 copy-start.13
  100.0 1.0 copy-start.15
  100.9 0.8 copy-start.17
  101.7 0.8 copy-start.19
  102.5 0.8 copy-start.21
  103.3 0.8 copy-start.23
  104.2 1.3 copy-start.7
  105.5 47.8 %all-to-all-start.3 = ((bf16[16,128,512]{2,1,0:T(8,128)(2,1)}), bf16[16,128,512]{2,1,0:T(8,128)(2,1)S(1)}, u32[]{:S(2)}, u32[]{:S(2)}) async-start(bf16[16,128,512]{2,1,0:T(8,128)(2,1)} %copy-done.9), calls=%async_computation.3 | async-start | bytes 4194304 | tf_op jit(solution)/shard_map/all_to_all | solution.py:364
  112.7 1.6 copy-start.8
  114.3 1.2 copy-start.11
  115.5 1.2 copy-start.14
  116.7 1.2 copy-start.16
  118.0 1.0 copy-start.18
  119.0 1.0 copy-start.20
  120.1 1.0 copy-start.22
  121.1 1.0 copy-start.24
  151.6 1.6 copy-start.6
  153.3 1.3 copy-start.2
  154.6 68.4 %all-to-all-start.2 = ((bf16[16,128,768]{2,1,0:T(8,128)(2,1)}), bf16[16,128,768]{2,1,0:T(8,128)(2,1)S(1)}, u32[]{:S(2)}, u32[]{:S(2)}) async-start(bf16[16,128,768]{2,1,0:T(8,128)(2,1)} %copy-done.6), calls=%async_computation.2 | async-start | bytes 6291456 | tf_op jit(solution)/shard_map/all_to_all | solution.py:364
  217.0 1.6 copy-start.3

commit v3 on v2

--- a/solution.py
+++ b/solution.py
@@ -16,10 +16,12 @@
 LOG2E = 1.4426950408889634
 NEG = -1e30
 ROPE_BASE = 1000000.0
+EXTRA = 8
 
 BF = jnp.bfloat16
 F32 = jnp.float32
 ANY = pl.BlockSpec(memory_space=pl.ANY)
+HBM = pl.BlockSpec(memory_space=pltpu.HBM)
 VM = pl.BlockSpec(memory_space=pltpu.VMEM)
 SM = pl.BlockSpec(memory_space=pltpu.SMEM)
 
@@ -30,6 +32,13 @@
 
 def cost(flops, nbytes):
     return pl.CostEstimate(flops=flops, bytes_accessed=nbytes, transcendentals=0)
+
+
+def run_copies(copies):
+    for copy in copies:
+        copy.start()
+    for copy in copies:
+        copy.wait()
 
 
 def pack_kernel(chunk, ways, proj, cot, out, buf, sem, out_sem):
@@ -74,7 +83,7 @@
             pltpu.SemaphoreType.DMA((ways, 4)),
             pltpu.SemaphoreType.DMA((ways,)),
         ],
-        compiler_params=params(8),
+        compiler_params=params(60),
         cost_estimate=cost(0, 4 * ways * rows * width),
         name=f"pack{chunk}",
     )(proj, cot)
@@ -197,8 +206,8 @@
             new.append(carry[h] + jnp.sum(g.astype(F32), 0, keepdims=True))
             for a in range(per):
                 part = slice(a * 128, (a + 1) * 128)
-                out[i * per + a, :, h * HEAD : (h + 1) * HEAD] = o[h * BLK + a * 128 : h * BLK + (a + 1) * 128]
-                out[i * per + a, :, 256 + h * HEAD : 256 + (h + 1) * HEAD] = g[part]
+                out[i * per + a, 0:128, h * HEAD : (h + 1) * HEAD] = o[h * BLK + a * 128 : h * BLK + (a + 1) * 128]
+                out[i * per + a, 0:128, 256 + h * HEAD : 256 + (h + 1) * HEAD] = g[part]
         return tuple(new)
 
     zero = jnp.zeros((1, HEAD), F32)
@@ -213,8 +222,8 @@
         rows = pl.ds(pl.multiple_of(b * 128, 128), 128)
         gk = unrope(dk[rows, :] * SCALE, cos[rows, :], sin[rows, :])
         gv = dv[rows, :]
-        out[b, :, 512:640] = gk.astype(BF)
-        out[b, :, 640:768] = gv.astype(BF)
+        out[b, 0:128, 512:640] = gk.astype(BF)
+        out[b, 0:128, 640:768] = gv.astype(BF)
         return (
             carry[0] + jnp.sum(gk, 0, keepdims=True),
             carry[1] + jnp.sum(gv, 0, keepdims=True),
@@ -234,7 +243,7 @@
     row = jax.ShapeDtypeStruct((n, HEAD), BF)
     col = jax.ShapeDtypeStruct((HEAD, n), BF)
     sums = jax.ShapeDtypeStruct((8, HEAD), F32)
-    out = jax.ShapeDtypeStruct((ways, n // ways, 768 if last else 512), BF)
+    out = jax.ShapeDtypeStruct((ways, n // ways + (EXTRA if last else 0), 768 if last else 512), BF)
     if last:
         args = (first_block, page, recv, *keys, cos, sin, first, bias, *state)
         outs = (out, sums)
@@ -254,7 +263,7 @@
     return pl.pallas_call(
         body,
         out_shape=outs,
-        in_specs=[SM, SM, ANY] + [VM] * (len(args) - 3),
+        in_specs=[SM, SM, HBM] + [VM] * (len(args) - 3),
         out_specs=tuple([VM] * len(outs)),
         scratch_shapes=scratch
         + [
@@ -265,40 +274,55 @@
             pltpu.VMEM((HEAD, 2 * BLK), F32),
             pltpu.SemaphoreType.DMA((3,)),
         ],
-        compiler_params=params(32),
+        compiler_params=params(60),
         cost_estimate=cost(20 * 10**9, 10**7),
         name="attend1" if last else "attend0",
     )(*args)
 
 
-def unpack_heads(recv, buf, att, gq, chunk, sem, out_sem):
-    ways = buf.shape[0]
-    fetch = [pltpu.make_async_copy(recv.at[d], buf.at[d], sem.at[d]) for d in range(ways)]
-    for copy in fetch:
-        copy.start()
-    stores = []
-    for d in range(ways):
+def sums_kernel(sums, _, out, rows, sem):
+    for r in range(6):
+        x = sums[r : r + 1, :]
+        hi = x.astype(BF).astype(F32)
+        mid = (x - hi).astype(BF).astype(F32)
+        low = x - hi - mid
+        rows[:, r * HEAD : (r + 1) * HEAD] = jnp.concatenate(
+            [hi, mid, low, jnp.zeros((EXTRA - 3, HEAD), F32)], 0
+        ).astype(BF)
+    run_copies(
+        [
+            pltpu.make_async_copy(rows, out.at[d, pl.ds(128, EXTRA), :], sem.at[d])
+            for d in range(out.shape[0])
+        ]
+    )
+
+
+def put_sums(sums, payload):
+    ways = payload.shape[0]
+    return pl.pallas_call(
+        sums_kernel,
+        out_shape=jax.ShapeDtypeStruct(payload.shape, payload.dtype),
+        in_specs=[VM, ANY],
+        out_specs=ANY,
+        input_output_aliases={1: 0},
+        scratch_shapes=[pltpu.VMEM((EXTRA, 768), BF), pltpu.SemaphoreType.DMA((ways,))],
+        compiler_params=params(60),
+        name="sums",
+    )(sums, payload)
+
+
+def head_copies(recv, att, gq, chunk, sem):
+    copies = []
+    for d in range(recv.shape[0]):
         cols = pl.ds(d * 512 + chunk * 256, 256)
-        fetch[d].wait()
-        stores.append(pltpu.make_async_copy(buf.at[d, :, pl.ds(0, 256)], att.at[:, cols], out_sem.at[d, 0]))
-        stores.append(pltpu.make_async_copy(buf.at[d, :, pl.ds(256, 256)], gq.at[:, cols], out_sem.at[d, 1]))
-        stores[-2].start()
-        stores[-1].start()
-    return stores
-
-
-def unpack0_kernel(recv, att, gq, buf, sem, out_sem):
-    for copy in unpack_heads(recv, buf, att, gq, 0, sem, out_sem):
-        copy.wait()
-
-
-def unpack_scratch(recv):
-    ways = recv.shape[0]
-    return [
-        pltpu.VMEM(recv.shape, BF),
-        pltpu.SemaphoreType.DMA((ways,)),
-        pltpu.SemaphoreType.DMA((ways, 2)),
-    ]
+        rows = pl.ds(0, 128)
+        copies.append(pltpu.make_async_copy(recv.at[d, rows, pl.ds(0, 256)], att.at[:, cols], sem.at[d, 0]))
+        copies.append(pltpu.make_async_copy(recv.at[d, rows, pl.ds(256, 256)], gq.at[:, cols], sem.at[d, 1]))
+    return copies
+
+
+def unpack0_kernel(recv, att, gq, sem):
+    run_copies(head_copies(recv, att, gq, 0, sem))
 
 
 def unpack0(recv):
@@ -307,27 +331,42 @@
     return pl.pallas_call(
         unpack0_kernel,
         out_shape=(shape, shape),
-        in_specs=[ANY],
+        in_specs=[VM],
         out_specs=(ANY, ANY),
-        scratch_shapes=unpack_scratch(recv),
-        compiler_params=params(8),
+        scratch_shapes=[pltpu.SemaphoreType.DMA((ways, 2))],
+        compiler_params=params(60),
         cost_estimate=cost(0, 4 * ways * rows * 512),
         name="unpack0",
     )(recv)
 
 
-def unpack1_kernel(recv, _a, _g, att, gq, kvg, buf, sem, out_sem):
-    ways = buf.shape[0]
-    stores = unpack_heads(recv, buf, att, gq, 1, sem, out_sem)
+def unpack1_kernel(recv, _a, _g, att, gq, kvg, gb, sem):
+    ways = recv.shape[0]
+    copies = head_copies(recv, att, gq, 1, sem)
+    for copy in copies:
+        copy.start()
     share = ways // KEY_VALUE_HEADS
+    qw = QUERY_HEADS * HEAD
     kw = KEY_VALUE_HEADS * HEAD
+
+    def sums_of(d):
+        t = recv[d, 128 : 128 + EXTRA, :].astype(F32)
+        return t[0:1] + t[1:2] + t[2:3]
+
     for h in range(KEY_VALUE_HEADS):
-        grad = buf[h * share, :, 512:768].astype(F32)
-        for r in range(1, share):
-            grad = grad + buf[h * share + r, :, 512:768].astype(F32)
+        grad = jnp.zeros((128, 256), F32)
+        kvsum = jnp.zeros((1, 256), F32)
+        for r in range(share):
+            d = h * share + r
+            grad = grad + recv[d, 0:128, 512:768].astype(F32)
+            b = sums_of(d)
+            gb[:, d * 512 : (d + 1) * 512] = b[:, 0:512]
+            kvsum = kvsum + b[:, 512:768]
         kvg[:, h * HEAD : (h + 1) * HEAD] = grad[:, :HEAD].astype(BF)
         kvg[:, kw + h * HEAD : kw + (h + 1) * HEAD] = grad[:, HEAD:].astype(BF)
-    for copy in stores:
+        gb[:, qw + h * HEAD : qw + (h + 1) * HEAD] = kvsum[:, :HEAD]
+        gb[:, qw + kw + h * HEAD : qw + kw + (h + 1) * HEAD] = kvsum[:, HEAD:]
+    for copy in copies:
         copy.wait()
 
 
@@ -340,11 +379,12 @@
             jax.ShapeDtypeStruct(att.shape, BF),
             jax.ShapeDtypeStruct(gq.shape, BF),
             jax.ShapeDtypeStruct((rows, 2 * KEY_VALUE_HEADS * HEAD), BF),
+            jax.ShapeDtypeStruct((1, (QUERY_HEADS + 2 * KEY_VALUE_HEADS) * HEAD), F32),
         ),
-        in_specs=[ANY, ANY, ANY],
-        out_specs=(ANY, ANY, VM),
+        in_specs=[VM, HBM, HBM],
+        out_specs=(HBM, HBM, VM, VM),
         input_output_aliases={1: 0, 2: 1},
-        scratch_shapes=unpack_scratch(recv),
+        scratch_shapes=[pltpu.SemaphoreType.DMA((ways, 2))],
         compiler_params=params(8),
         cost_estimate=cost(0, 4 * ways * rows * 768),
         name="unpack1",
@@ -397,15 +437,10 @@
         True, ways, first_block, page, recv1.reshape(n, 512), cos, sin, first, qbias[2:4],
         (k, v, kt, vt), (dk, dv, sums),
     )
-    recv3 = exchange(send3)
-    sums = lax.all_gather(lax.psum(sums, "dp"), "sp")
+    recv3 = exchange(put_sums(lax.psum(sums, "dp"), send3))
     att, gq = unpack0(recv2)
-    att, gq, kvg = unpack1(recv3, att, gq)
-    kv_sums = jnp.sum(sums[:, 4:6].reshape(KEY_VALUE_HEADS, share, 2, HEAD), 1)
-    gb = jnp.concatenate(
-        [sums[:, 0:4].reshape(-1), kv_sums[:, 0].reshape(-1), kv_sums[:, 1].reshape(-1)]
-    )
-    return att, gq, kvg, gb
+    att, gq, kvg, gb = unpack1(recv3, att, gq)
+    return att, gq, kvg, gb.reshape(-1)
 
 
 def solution(mesh):

time: 226 us -> 211 us (0.934); the launches traced: 230 us -> 209 us
  waiting for transfers between devices: 36.9 us -> 82.4 us
  blocking collectives: 54.5 us -> 12.4 us
  local copies, waits for them, and re-layouts: 29.5 us -> 3.47 us
    all_to_all x4, waiting for transfers between devices: 36.9 us -> 82.4 us  [exchange(): return lax.all_to_all(x, 'sp', split_axis=0, concat_axis=0, tiled=True)]
    all_gather x1 -> x0, blocking collectives: 43.9 us -> none  [shards(): sums = lax.all_gather(lax.psum(sums, 'dp'), 'sp')]
    unnamed x52 -> x8, local copies, waits for them, and re-layouts: 27.9 us -> 1.37 us
    pallas_call x3 -> x4, Pallas kernels: 64 us -> 68.4 us  [the longest x2 63.7 us: attend(): pl.pallas_call(body, out_shape=outs, in_specs=[SM, SM, HBM] + [VM] * (len...]
    pallas_call x1, Pallas kernels: 6.56 us -> 2.36 us  [unpack1(): pl.pallas_call(unpack1_kernel, out_shape=(jax.ShapeDtypeStruct(att.shape,...]
  transfers between devices with their start and end apart: 4 -> 4, of which waited for: 1 -> 2; matrix products, arithmetic and copies ran while one was open for 3% -> 4% of each run, Pallas kernels for 29% -> 34%
where the time goes in v3:
time: 211 us; the launch traced here: 209 us
  waiting for transfers between devices  82.4 us (39%)
  Pallas kernels  77.5 us (37%)
  starting transfers between devices  25.6 us (12%)
  blocking collectives  12.4 us (6%)
  other arithmetic  7.07 us (3%)
  local copies, waits for them, and re-layouts  3.47 us (2%)
    all_to_all x4, waiting for transfers between devices, exchange(): return lax.all_to_all(x, 'sp', split_axis=0, concat_axis=0, tiled=True)  82.4 us
    pallas_call x2, Pallas kernels, attend(): pl.pallas_call(body, out_shape=outs, in_specs=[SM, SM, HBM] + [VM] * (len...  63.7 us
    all_to_all x4, starting transfers between devices, exchange(): return lax.all_to_all(x, 'sp', split_axis=0, concat_axis=0, tiled=True)  25.6 us
    psum x1, blocking collectives, shards(): recv3 = exchange(put_sums(lax.psum(sums, 'dp'), send3))  12.4 us
    pallas_call x2, Pallas kernels, pack(): pl.pallas_call(functools.partial(pack_kernel, chunk, ways), out_shape=jax...  6.72 us
    mul x1, other arithmetic, rope_tables(): return (jnp.cos(angles), jnp.sin(angles) * sign[None, :])  5.63 us
  transfers between devices with their start and end apart: 4, of which 2 were waited for; matrix products, arithmetic and copies ran while one was open for 4% of the time, Pallas kernels for 34%

profile of v3, /device:TPU:64, one launch (start us, length us, event | category | flops | bytes accessed | tf_op | source)
XLA Modules:
  0.0 209.2 jit_solution(3082935317494335758)
XLA Ops:
  0.6 3.8 %pack0.1 = bf16[16,128,768]{2,1,0:T(8,128)(2,1)} custom-call(bf16[128,10240]{1,0:T(8,128)(2,1)} %proj.3, bf16[128,8192]{1,0:T(8,128)(2,1)} %cot.3), custom_call_target="tpu_custom_call" | custom-call | bytes 6291456 | tf_op jit(solution)/shard_map/pack0/pallas_call | solution.py:76
  4.4 7.0 %all-to-all-start.1 = ((bf16[16,128,768]{2,1,0:T(8,128)(2,1)}), bf16[16,128,768]{2,1,0:T(8,128)(2,1)S(1)}, u32[]{:S(2)}, u32[]{:S(2)}) async-start(bf16[16,128,768]{2,1,0:T(8,128)(2,1)} %pack0.1), calls=%async_computation.1 | async-start | bytes 6291456 | tf_op jit(solution)/shard_map/all_to_all | solution.py:404
  11.5 0.0 copy-start.3
  11.5 3.0 %pack1.1 = bf16[16,128,512]{2,1,0:T(8,128)(2,1)} custom-call(bf16[128,10240]{1,0:T(8,128)(2,1)} %proj.3, bf16[128,8192]{1,0:T(8,128)(2,1)} %cot.3), custom_call_target="tpu_custom_call" | custom-call | bytes 4194304 | tf_op jit(solution)/shard_map/pack1/pallas_call | solution.py:76
  14.5 0.0 copy-done.3
  14.5 0.2 reduce-window_clone.1
  14.7 0.1 select_reduce_fusion
  14.8 0.0 copy-start.2
  14.8 0.7 constant_dynamic-slice_fusion.1
  15.5 0.7 constant_dynamic-slice_fusion.2
  16.2 0.1 slice_reduce_fusion
  16.3 0.6 and_select_fusion.1.refs_0_
  16.9 0.6 fusion.5
  17.5 5.6 %fusion = (f32[2048,128]{1,0:T(8,128)}, f32[2048,128]{1,0:T(8,128)}) fusion(f32[128]{0:T(128)S(1)} %get-tuple-element.42, f32[128]{0:T(128)S(1)} %get-tuple-element.43, f32[2048]{0:T(1024)S(1)} %subtract_convert_fusion), kind=kLoop, calls=%fused_computation.2 | loop fusion | flops 524288 | bytes 2106368 | tf_op jit(solution)/shard_map/mul | solution.py:400
  23.1 36.0 %all-to-all-done.1 = bf16[16,128,768]{2,1,0:T(8,128)(2,1)S(1)} async-done(((bf16[16,128,768]{2,1,0:T(8,128)(2,1)}), bf16[16,128,768]{2,1,0:T(8,128)(2,1)S(1)}, u32[]{:S(2)}, u32[]{:S(2)}) %all-to-all-start.1) | async-done | bytes 3145760 | tf_op jit(solution)/shard_map/all_to_all | solution.py:404
  59.1 0.0 copy-start.1
  59.1 0.0 copy-done.2
  59.1 4.4 %all-to-all-start = ((bf16[16,128,512]{2,1,0:T(8,128)(2,1)}), bf16[16,128,512]{2,1,0:T(8,128)(2,1)}, u32[]{:S(2)}, u32[]{:S(2)}) async-start(bf16[16,128,512]{2,1,0:T(8,128)(2,1)} %pack1.1), calls=%async_computation | async-start | bytes 4194304 | tf_op jit(solution)/shard_map/all_to_all | solution.py:404
  63.6 0.0 copy-done.1
  63.6 0.6 pad_maximum_fusion.refs_6_
  64.1 31.8 %attend0.1 = (bf16[16,128,512]{2,1,0:T(8,128)(2,1)}, bf16[2048,128]{1,0:T(8,128)(2,1)}, bf16[2048,128]{1,0:T(8,128)(2,1)}, bf16[128,2048]{1,0:T(8,128)(2,1)}, bf...) custom-call(s32[8]{0:T(128)} %and_select_fusion.1.refs_0_, ...), custom_call_target="tpu_custom_call" | custom-call | flops 20000000000 | bytes 10000000 | tf_op jit(solution)/shard_map/attend0/pallas_call | solution.py:263
  95.9 0.0 all-to-all-done
  96.0 7.1 %all-to-all-start.3 = ((bf16[16,128,512]{2,1,0:T(8,128)(2,1)}), bf16[16,128,512]{2,1,0:T(8,128)(2,1)S(1)}, u32[]{:S(2)}, u32[]{:S(2)}) async-start(bf16[16,128,512]{2,1,0:T(8,128)(2,1)} %get-tuple-element.29), calls=%async_computation.3 | async-start | bytes 4194304 | tf_op jit(solution)/shard_map/all_to_all | solution.py:404
  103.1 31.8 %attend1.1 = (bf16[16,136,768]{2,1,0:T(8,128)(2,1)}, f32[8,128]{1,0:T(8,128)}) custom-call(s32[8]{0:T(128)} %and_select_fusion.1.refs_0_, s32[128]{0:T(128)} %bitcast.15, bf16[2048,512]{1,0:T(8,128)(2,1)} %bitcast.2.refs_2_, bf16[2048,128]{1,0:T(8,128)(2,1)} %get-tuple-element.20.refs_3_, bf16[2048,128]{1,0:T(8,128)(2,1)} %get-tuple-element.21.refs_4_, ...), custom_call_target="tpu_custom_call" | custom-call | flops 20000000000 | bytes 10000000 | tf_op jit(solution)/shard_map/attend1/pallas_call | solution.py:263
  135.0 12.4 %psum.7.sums = f32[8,128]{1,0:T(8,128)} all-reduce(f32[8,128]{1,0:T(8,128)} %get-tuple-element.27), channel_id=1, replica_groups=mesh['dp'=8,'sp'=16] {'dp'}, use_global_device_ids=true, to_apply=%region_2.3 | all-reduce | flops 1024 | bytes 8192 | tf_op jit(solution)/shard_map/psum | solution.py:440
  147.3 1.5 sums.1
  148.9 0.0 all-to-all-done.3.recv
  148.9 0.0 copy-start
  148.9 1.3 copy-done
  150.3 6.9 %all-to-all-start.2 = ((bf16[16,136,768]{2,1,0:T(8,128)(2,1)}), bf16[16,136,768]{2,1,0:T(8,128)(2,1)S(1)}, u32[]{:S(2)}, u32[]{:S(2)}) async-start(bf16[16,136,768]{2,1,0:T(8,128)(2,1)} %sums.1), calls=%async_computation.2 | async-start | bytes 6684672 | tf_op jit(solution)/shard_map/all_to_all | solution.py:404
  157.2 3.2 %unpack0.1 = (bf16[128,8192]{1,0:T(8,128)(2,1)}, bf16[128,8192]{1,0:T(8,128)(2,1)}) custom-call(bf16[16,128,512]{2,1,0:T(8,128)(2,1)} %copy-done), custom_call_target="tpu_custom_call" | custom-call | bytes 4194304 | tf_op jit(solution)/shard_map/unpack0/pallas_call | solution.py:331
  160.4 46.4 %all-to-all-done.2.recv = bf16[16,136,768]{2,1,0:T(8,128)(2,1)S(1)} async-done(((bf16[16,136,768]{2,1,0:T(8,128)(2,1)}), bf16[16,136,768]{2,1,0:T(8,128)(2,1)S(1)}, u32[]{:S(2)}, u32[]{:S(2)}) %all-to-all-start.2) | async-done | bytes 3342368 | tf_op jit(solution)/shard_map/all_to_all | solution.py:404
  206.8 2.4 %unpack1.1 = (bf16[128,8192]{1,0:T(8,128)(2,1)}, bf16[128,8192]{1,0:T(8,128)(2,1)}, bf16[128,2048]{1,0:T(8,128)(2,1)}, f32[1,10240]{1,0:T(1,128)}) custom-call(bf16[16,136,768]{2,1,0:T(8,128)(2,1)S(1)} %all-to-all-done.2.recv, bf16[128,8192]{1,0:T(8,128)(2,1)} %get-tuple-element.30._a, ...), custom_call_target="tpu_custom_call", output_to_operand_aliasing={{0}: (1, {}), {1}: (2, {})} | custom-call | bytes 6291456 | tf_op jit(solution)/shard_map/unpack1/pallas_call | solution.py:376
  (4 shorter events, 0.0 us)
Async XLA Ops:
  4.4 54.7 %all-to-all-start.1 = ((bf16[16,128,768]{2,1,0:T(8,128)(2,1)}), bf16[16,128,768]{2,1,0:T(8,128)(2,1)S(1)}, u32[]{:S(2)}, u32[]{:S(2)}) async-start(bf16[16,128,768]{2,1,0:T(8,128)(2,1)} %pack0.1), calls=%async_computation.1 | async-start | bytes 6291456 | tf_op jit(solution)/shard_map/all_to_all | solution.py:404
  11.5 3.0 %copy-start.3 = (s32[1,4]{1,0:T(1,128)S(1)}, s32[1,4]{1,0:T(1,128)}, u32[]{:S(2)}) copy-start(s32[1,4]{1,0:T(1,128)} %param.8) | copy-start | bytes 52
  14.8 44.3 %copy-start.2 = (s32[2048]{0:T(1024)}, s32[2048]{0:T(1024)S(1)}, u32[]{:S(2)}) copy-start(s32[2048]{0:T(1024)S(1)} %select_reduce_fusion) | copy-start | bytes 24580
  59.1 4.5 %copy-start.1 = (bf16[16,128,768]{2,1,0:T(8,128)(2,1)}, bf16[16,128,768]{2,1,0:T(8,128)(2,1)S(1)}, u32[]{:S(2)}) copy-start(bf16[16,128,768]{2,1,0:T(8,128)(2,1)S(1)} %all-to-all-done.1) | copy-start | bytes 9437188
  59.1 36.8 %all-to-all-start = ((bf16[16,128,512]{2,1,0:T(8,128)(2,1)}), bf16[16,128,512]{2,1,0:T(8,128)(2,1)}, u32[]{:S(2)}, u32[]{:S(2)}) async-start(bf16[16,128,512]{2,1,0:T(8,128)(2,1)} %pack1.1), calls=%async_computation | async-start | bytes 4194304 | tf_op jit(solution)/shard_map/all_to_all | solution.py:404
  96.0 52.9 %all-to-all-start.3 = ((bf16[16,128,512]{2,1,0:T(8,128)(2,1)}), bf16[16,128,512]{2,1,0:T(8,128)(2,1)S(1)}, u32[]{:S(2)}, u32[]{:S(2)}) async-start(bf16[16,128,512]{2,1,0:T(8,128)(2,1)} %get-tuple-element.29), calls=%async_computation.3 | async-start | bytes 4194304 | tf_op jit(solution)/shard_map/all_to_all | solution.py:404
  148.9 1.4 copy-start
  150.3 56.5 %all-to-all-start.2 = ((bf16[16,136,768]{2,1,0:T(8,128)(2,1)}), bf16[16,136,768]{2,1,0:T(8,128)(2,1)S(1)}, u32[]{:S(2)}, u32[]{:S(2)}) async-start(bf16[16,136,768]{2,1,0:T(8,128)(2,1)} %sums.1), calls=%async_computation.2 | async-start | bytes 6684672 | tf_op jit(solution)/shard_map/all_to_all | solution.py:404
